TPU v7x, 128 devices: a whole 4x4x4 slice. The times are simulated.
128 devices in a mesh: ulysses: 8 (over z, core), dp: 16 (over x, y).
Axes of the slice: x: 4, y: 4, z: 4, core: 2. Of those that a mesh axis runs over, the one named last changes fastest.
Arguments:
- tokens: bfloat16 [16, 2048, 2048], P('dp', 'ulysses'), may hold values from -60 to 60
- d_out: bfloat16 [16, 2048, 2048], P('dp', 'ulysses'), may hold values from -6 to 6
- lengths: int32 [16, 21], P('dp'), may hold values from 1 to 384, 2048 in all within a row
- gain: bfloat16 [2048], P('dp'), may hold values from 0.5 to 1.5
- w_qkv: bfloat16 [2048, 1536], P('dp'), may hold values from -16 to 16
- w_out: bfloat16 [2048, 1024], P('dp'), may hold values from -0.1875 to 0.1875
Outputs:
- d_tokens: bfloat16 [16, 2048, 2048], P('dp', 'ulysses')
- d_w_qkv: float32 [2048, 1536], P(('ulysses', 'dp'))
- d_w_out: float32 [2048, 1024], P(('ulysses', 'dp'))
- d_gain: float32 [2048], P(('ulysses', 'dp'))
Inputs may be any that keep to these rules, and one draw needn't show every extreme that they name: Each row holds whole document lengths of 1 to 384 tokens that sum to 2048; the longest is exactly 384.
All inputs are finite; a program needn't handle non-finite values.
Results may differ from a plain program's by a relative error of at most 0.01.
The roundings to bfloat16 on the way count: a program that leaves them out, or rounds other values in their place, can miss the bound.
Values may be sent and summed in bfloat16 or wider, within the bound.
A program may use at most 128 MiB of HBM per device.

v0:
```python
import math

import jax
import jax.numpy as jnp
from jax import lax
from jax.sharding import PartitionSpec as P

HEADS = 16
KV_HEADS = 4
HEAD_DIM = 64
QW = 1024
KW = 256


EPS = 1e-05
ROPE_BASE = 500000.0


def doc_positions(doc_lengths, length):
    bounds = jnp.cumsum(doc_lengths) - doc_lengths
    places = jnp.arange(length, dtype=jnp.int32)
    begins = jnp.max(jnp.where(bounds[None, :] <= places[:, None], bounds[None, :], 0), axis=1)
    return (begins, places - begins)


def rotary_tables(places):
    inverse = ROPE_BASE ** (-jnp.arange(0, HEAD_DIM, 2).astype(jnp.float32) / HEAD_DIM)
    angles = places.astype(jnp.float32)[:, None] * inverse[None, :]
    angles = jnp.concatenate([angles, angles], axis=1)
    return (jnp.cos(angles), jnp.sin(angles))


def rotate(values, cos_table, sin_table):
    half_dim = HEAD_DIM // 2
    turned = jnp.concatenate([-values[..., half_dim:], values[..., :half_dim]], axis=-1)
    return values * cos_table[:, None, :] + turned * sin_table[:, None, :]


def attend(query_head, key_head, value_head, grad_head, begins):
    length, heads_here, _ = query_head.shape
    block_len = min(512, length)
    blocks = length // block_len
    scale = HEAD_DIM ** (-0.5)
    filler = jnp.zeros((block_len, HEAD_DIM), key_head.dtype)
    key_blocks = jnp.concatenate([filler, key_head], axis=0).reshape(
        blocks + 1, block_len, HEAD_DIM
    )
    key_window = jnp.concatenate([key_blocks[:-1], key_blocks[1:]], axis=1)
    value_blocks = jnp.concatenate([filler, value_head], axis=0).reshape(
        blocks + 1, block_len, HEAD_DIM
    )
    value_window = jnp.concatenate([value_blocks[:-1], value_blocks[1:]], axis=1)
    query_blocks = query_head.reshape(blocks, block_len * heads_here, HEAD_DIM)
    grad_blocks = grad_head.reshape(blocks, block_len * heads_here, HEAD_DIM)
    begin_blocks = begins.reshape(blocks, block_len)

    def one_block(inputs):
        block_index, query_b, grad_b, key_w, value_w, begin_b = inputs
        query_pos = block_index * block_len + jnp.arange(block_len, dtype=jnp.int32)
        key_pos = (block_index - 1) * block_len + jnp.arange(2 * block_len, dtype=jnp.int32)
        allowed = (key_pos[None, :] >= begin_b[:, None]) & (key_pos[None, :] <= query_pos[:, None])
        allowed = jnp.broadcast_to(allowed[:, None, :], (block_len, heads_here, 2 * block_len))
        allowed = allowed.reshape(block_len * heads_here, 2 * block_len)
        scores = jnp.einsum("qd,kd->qk", query_b, key_w, preferred_element_type=jnp.float32) * scale
        scores = jnp.where(allowed, scores, -1e30)
        peak = jnp.max(scores, axis=1, keepdims=True)
        weights = jnp.where(allowed, jnp.exp(scores - peak), 0.0)
        shares = weights / jnp.sum(weights, axis=1, keepdims=True)
        shares_low = shares.astype(jnp.bfloat16)
        mixed = jnp.dot(shares_low, value_w, preferred_element_type=jnp.float32)
        row_dot = jnp.sum(grad_b.astype(jnp.float32) * mixed, axis=1, keepdims=True)
        d_shares = jnp.einsum("qd,kd->qk", grad_b, value_w, preferred_element_type=jnp.float32)
        d_scores = (shares * (d_shares - row_dot) * scale).astype(jnp.bfloat16)
        d_query = jnp.dot(d_scores, key_w, preferred_element_type=jnp.float32)
        d_keys = jnp.einsum("qk,qd->kd", d_scores, query_b, preferred_element_type=jnp.float32)
        d_values = jnp.einsum("qk,qd->kd", shares_low, grad_b, preferred_element_type=jnp.float32)
        return (mixed.astype(jnp.bfloat16), d_query, d_keys, d_values)

    block_ids = jnp.arange(blocks, dtype=jnp.int32)
    mixed, d_query, d_keys, d_values = lax.map(
        one_block, (block_ids, query_blocks, grad_blocks, key_window, value_window, begin_blocks)
    )
    mixed = mixed.reshape(length, heads_here * HEAD_DIM)
    d_query = d_query.reshape(length, heads_here, HEAD_DIM)
    pad_front = ((1, 0), (0, 0), (0, 0))
    pad_back = ((0, 1), (0, 0), (0, 0))
    d_keys = (jnp.pad(d_keys[:, :block_len], pad_back) + jnp.pad(d_keys[:, block_len:], pad_front))[
        1:
    ]
    d_values = (
        jnp.pad(d_values[:, :block_len], pad_back) + jnp.pad(d_values[:, block_len:], pad_front)
    )[1:]
    return (mixed, d_query, d_keys.reshape(length, HEAD_DIM), d_values.reshape(length, HEAD_DIM))


def body(tokens, d_out, lengths, gain, w_qkv, w_out):
    groups = lax.axis_size("ulysses")
    member = lax.axis_index("ulysses")
    full_qkv, full_out, full_gain = (
        lax.all_gather(w_qkv, "dp", axis=0, tiled=True),
        lax.all_gather(w_out, "dp", axis=0, tiled=True),
        lax.all_gather(gain, "dp", axis=0, tiled=True),
    )
    token_rows = tokens[0]
    grad_rows = d_out[0]
    local_rows = token_rows.shape[0]
    length = local_rows * groups
    heads_here = HEADS // groups
    repeat = groups // KV_HEADS
    q_width = heads_here * HEAD_DIM
    factor = 1.0 / math.sqrt(length * lax.axis_size("dp"))
    begins, places = doc_positions(lengths[0], length)
    local_places = lax.dynamic_slice_in_dim(places, member * local_rows, local_rows)
    gain_wide = full_gain.astype(jnp.float32)
    wide_rows = token_rows.astype(jnp.float32)
    inv_rms = lax.rsqrt(jnp.mean(wide_rows * wide_rows, axis=1, keepdims=True) + EPS)
    unit_rows = wide_rows * inv_rms
    normed = (unit_rows * gain_wide[None, :]).astype(jnp.bfloat16)
    projected = jnp.dot(normed, full_qkv, preferred_element_type=jnp.float32)
    cos_local, sin_local = rotary_tables(local_places)
    query = rotate(
        projected[:, :QW].reshape(local_rows, HEADS, HEAD_DIM), cos_local, sin_local
    ).astype(jnp.bfloat16)
    key_rows = rotate(
        projected[:, QW : QW + KW].reshape(local_rows, KV_HEADS, HEAD_DIM), cos_local, sin_local
    ).astype(jnp.bfloat16)
    value_rows = (
        projected[:, QW + KW :].astype(jnp.bfloat16).reshape(local_rows, KV_HEADS, HEAD_DIM)
    )
    key_rows = jnp.repeat(key_rows, repeat, axis=1)
    value_rows = jnp.repeat(value_rows, repeat, axis=1)
    d_attn = jnp.dot(grad_rows, full_out, preferred_element_type=jnp.float32).astype(jnp.bfloat16)
    packed = jnp.concatenate(
        [
            query.reshape(local_rows, groups, q_width),
            key_rows,
            value_rows,
            d_attn.reshape(local_rows, groups, q_width),
        ],
        axis=2,
    )
    arrived = lax.all_to_all(packed, "ulysses", split_axis=1, concat_axis=0, tiled=True)
    head_block = arrived[:, 0, :]
    query_head = head_block[:, :q_width].reshape(length, heads_here, HEAD_DIM)
    key_head = head_block[:, q_width : q_width + HEAD_DIM]
    value_head = head_block[:, q_width + HEAD_DIM : q_width + 2 * HEAD_DIM]
    grad_head = head_block[:, q_width + 2 * HEAD_DIM :].reshape(length, heads_here, HEAD_DIM)
    mixed, d_query, d_keys, d_values = attend(query_head, key_head, value_head, grad_head, begins)
    cos_table, sin_table = rotary_tables(places)
    d_query = rotate(d_query, cos_table, -sin_table).astype(jnp.bfloat16).reshape(length, q_width)
    d_keys = rotate(d_keys[:, None, :], cos_table, -sin_table)[:, 0, :].astype(jnp.bfloat16)
    d_values = d_values.astype(jnp.bfloat16)
    outgoing = jnp.concatenate([mixed, d_query, d_keys, d_values], axis=1)[:, None, :]
    returned = lax.all_to_all(outgoing, "ulysses", split_axis=0, concat_axis=1, tiled=True)
    mixed_rows = returned[:, :, :q_width].reshape(local_rows, QW)
    dq_rows = returned[:, :, q_width : 2 * q_width].reshape(local_rows, QW)
    dk_rows = returned[:, :, 2 * q_width : 2 * q_width + HEAD_DIM].astype(jnp.float32)
    dk_rows = (
        dk_rows.reshape(local_rows, KV_HEADS, repeat, HEAD_DIM)
        .sum(axis=2)
        .astype(jnp.bfloat16)
        .reshape(local_rows, KW)
    )
    dv_rows = returned[:, :, 2 * q_width + HEAD_DIM :].astype(jnp.float32)
    dv_rows = (
        dv_rows.reshape(local_rows, KV_HEADS, repeat, HEAD_DIM)
        .sum(axis=2)
        .astype(jnp.bfloat16)
        .reshape(local_rows, KW)
    )
    d_proj = jnp.concatenate([dq_rows, dk_rows, dv_rows], axis=1)
    grad_qkv = jnp.einsum("td,tc->dc", normed, d_proj, preferred_element_type=jnp.float32) * factor
    grad_out = (
        jnp.einsum("td,tc->dc", grad_rows, mixed_rows, preferred_element_type=jnp.float32) * factor
    )
    d_normed = jnp.einsum("tc,dc->td", d_proj, full_qkv, preferred_element_type=jnp.float32)
    grad_gain = jnp.sum(d_normed * unit_rows, axis=0) * factor
    scaled = d_normed * gain_wide[None, :]
    d_rows = inv_rms * (scaled - unit_rows * jnp.mean(scaled * unit_rows, axis=1, keepdims=True))
    d_tokens = (grad_rows.astype(jnp.float32) + d_rows).astype(jnp.bfloat16)
    summed = (
        lax.psum_scatter(grad_qkv, ("ulysses", "dp"), scatter_dimension=0, tiled=True),
        lax.psum_scatter(grad_out, ("ulysses", "dp"), scatter_dimension=0, tiled=True),
        lax.psum_scatter(grad_gain, ("ulysses", "dp"), scatter_dimension=0, tiled=True),
    )
    return (d_tokens[None], summed[0], summed[1], summed[2])


def solution(mesh):
    in_specs = (
        P("dp", "ulysses", None),
        P("dp", "ulysses", None),
        P("dp", None),
        P("dp"),
        P("dp", None),
        P("dp", None),
    )
    out_specs = (
        P("dp", "ulysses", None),
        P(("ulysses", "dp"), None),
        P(("ulysses", "dp"), None),
        P(("ulysses", "dp")),
    )
    return jax.shard_map(body, mesh=mesh, in_specs=in_specs, out_specs=out_specs, check_vma=False)
```

profile of v0, /device:TPU:1, one launch (start us, length us, event | category | flops | bytes accessed | tf_op | source)
XLA Modules:
  0.0 1205.1 jit_solution(16550320424071945293)
XLA Ops:
  9.5 17.3 %all-gather = bf16[16,1,128]{2,1,0:T(2,128)(2,1)S(1)} all-gather(bf16[1,1,128]{2,1,0:T(2,128)(2,1)} %bitcast.199), channel_id=1, replica_groups=mesh['ulysses'=8,'dp'=16] {'dp'}, dimensions={0}, use_global_device_ids=true | all-gather | bytes 4352 | tf_op jit(solution)/shard_map/all_gather | solution.py:102
  29.5 35.0 %all-gather.6.cloned.1.call-done = bf16[2048,1024]{1,0:T(8,128)(2,1)} async-done(((bf16[128,1024]{1,0:T(8,128)(2,1)}), bf16[2048,1024]{1,0:T(8,128)(2,1)}) %all-gather.6.cloned.1.call-update) | async-done | bytes 4194320 | tf_op jit(solution)/shard_map/all_gather | solution.py:101
  64.5 3.8 convolution_convert_fusion
  68.4 59.1 %all-gather.4.cloned.1.call-done = bf16[2048,1536]{1,0:T(8,128)(2,1)} async-done(((bf16[128,1536]{1,0:T(8,128)(2,1)}), bf16[2048,1536]{1,0:T(8,128)(2,1)}) %all-gather.4.cloned.1.call-update) | async-done | bytes 6291472 | tf_op jit(solution)/shard_map/all_gather | solution.py:100
  127.5 4.6 fusion.58
  134.9 5.3 all-to-all-start
  140.3 20.4 %all-to-all-done = bf16[256,8,384]{0,2,1:T(8,128)(2,1)S(1)} async-done(((bf16[256,8,384]{0,2,1:T(8,128)(2,1)}), bf16[256,8,384]{0,2,1:T(8,128)(2,1)S(1)}, u32[]{:S(2)}, u32[]{:S(2)}) %all-to-all-start) | async-done | bytes 1572896 | tf_op jit(solution)/shard_map/all_to_all | solution.py:142
  169.7 78.8 %while.18 = (s32[]{:T(128)}, bf16[4,1024,64]{1,2,0:T(8,128)(2,1)}, f32[4,1024,64]{1,2,0:T(8,128)}, f32[4,1024,64]{1,2,0:T(8,128)}, f32[4,1024,64]{1,2,0:T(8,128)...) while((s32[]{:T(128)}, bf16[4,1024,64]{1,2,0:T(8,128)(2,1)}, ...), condition=%wide.region_7.8_spmd, body=%wide.region_3.7_spmd.sunk | while | flops 837548544 | bytes 50663740 | solution.py:80
  174.5 2.6 reshape.350
  194.0 2.6 reshape.350
  213.6 2.6 reshape.350
  233.1 2.6 reshape.350
  260.5 2.3 slice_negate_fusion
  262.8 2.5 maximum_multiply_fusion
  273.8 24.7 %all_to_all.33 = bf16[8,2,49152]{2,1,0:T(2,128)(2,1)} all-to-all(bf16[8,2,49152]{2,1,0:T(2,128)(2,1)S(1)} %reshape.347), channel_id=1, replica_groups=mesh['ulysses'=8,'dp'=16] {'ulysses'}, dimensions={0} | all-to-all | bytes 3145728 | tf_op jit(solution)/shard_map/all_to_all | solution.py:154
  298.4 4.7 reshape.348
  305.2 4.5 multiply_bitcast_fusion
  309.7 9.2 copy.184
  322.8 6.5 convolution_multiply_fusion
  330.2 6.3 fusion.44
  336.5 65.3 %all-reduce.6 = f32[2048]{0:T(1024)S(1)} all-reduce(f32[2048]{0:T(1024)S(1)} %broadcast_multiply_fusion.2), channel_id=4, replica_groups=mesh['ulysses'=8,'dp'=16] {'ulysses','dp'}, use_global_device_ids=true, to_apply=%region_14.15.clone | all-reduce | flops 2048 | bytes 16384
  402.4 3.2 fusion.46
  405.6 541.3 %reduce-scatter.7.cloned.1.call-done = f32[16,1024]{1,0:T(8,128)} async-done(((f32[2048,1024]{1,0:T(8,128)}), f32[16,1024]{1,0:T(8,128)}) %reduce-scatter.7.cloned.1.call-update) | async-done | bytes 65552
  946.9 251.4 %reduce-scatter.5.cloned.1.call-done = f32[16,1536]{1,0:T(8,128)} async-done(((f32[2048,1536]{1,0:T(8,128)}), f32[16,1536]{1,0:T(8,128)}) %reduce-scatter.5.cloned.1.call-update) | async-done | bytes 98320 | tf_op jit(solution)/shard_map/reduce_scatter | solution.py:182
  (220 shorter events, 106.5 us)
Async XLA Ops:
  7.2 57.3 %all-gather.6.cloned.1.call-start = ((), (), s32[]{:S(2)}) async-start(), calls=%async_computation.5 | async-start | bytes 4456448 | tf_op jit(solution)/shard_map/all_gather | solution.py:101
  7.9 119.6 %all-gather.4.cloned.1.call-start = ((), (), s32[]{:S(2)}) async-start(), calls=%async_computation.4 | async-start | bytes 6684672 | tf_op jit(solution)/shard_map/all_gather | solution.py:100
  26.8 100.7 %copy-start.21 = (f32[16,1,128]{2,1,0:T(1,128)}, f32[16,1,128]{2,1,0:T(1,128)S(1)}, u32[]{:S(2)}) copy-start(f32[16,1,128]{2,1,0:T(1,128)S(1)} %convert_element_type.126) | copy-start | bytes 24580
  29.4 98.1 %copy-start.23 = (f32[256]{0:T(256)}, f32[256]{0:T(256)S(1)}, u32[]{:S(2)}) copy-start(f32[256]{0:T(256)S(1)} %add_rsqrt_fusion) | copy-start | bytes 3076
  29.5 98.1 %copy-start.2 = (bf16[1,256,2048]{2,1,0:T(8,128)(2,1)S(1)}, bf16[1,256,2048]{2,1,0:T(8,128)(2,1)}, u32[]{:S(2)}) copy-start(bf16[1,256,2048]{2,1,0:T(8,128)(2,1)} %param.8) | copy-start | bytes 3145732
  134.9 25.8 %all-to-all-start = ((bf16[256,8,384]{0,2,1:T(8,128)(2,1)}), bf16[256,8,384]{0,2,1:T(8,128)(2,1)S(1)}, u32[]{:S(2)}, u32[]{:S(2)}) async-start(bf16[256,8,384]{0,2,1:T(8,128)(2,1)} %pad_maximum_fusion), calls=%async_computation | async-start | bytes 3145728 | tf_op jit(solution)/shard_map/all_to_all | solution.py:142
  140.1 806.7 %reduce-scatter.7.cloned.1.call-start = ((), (), s32[]{:S(2)}) async-start(), calls=%async_computation.7 | async-start | bytes 8454144
  162.9 2.9 copy-start.14
  180.8 2.2 copy-start.10
  200.3 2.2 copy-start.10
  219.8 2.2 copy-start.10
  239.4 2.2 copy-start.10
  248.5 2.4 copy-start.20
  249.9 2.8 copy-start.17
  255.8 3.7 copy-start.15
  260.5 2.4 copy-start.9
  267.4 1.6 copy-start.8
  303.4 1.8 copy-start.6
  319.0 3.8 copy-start.3
  319.0 3.8 copy-start.22
  319.0 3.8 copy-start.24
  319.0 879.3 %reduce-scatter.5.cloned.1.call-start = ((), (), s32[]{:S(2)}) async-start(), calls=%async_computation.6 | async-start | bytes 12681216 | tf_op jit(solution)/shard_map/reduce_scatter | solution.py:182
  322.5 6.7 copy-start.18
  330.2 72.2 %copy-start.7 = (bf16[1,256,2048]{2,1,0:T(8,128)(2,1)S(1)}, bf16[1,256,2048]{2,1,0:T(8,128)(2,1)}, u32[]{:S(2)}) copy-start(bf16[1,256,2048]{2,1,0:T(8,128)(2,1)} %param.9) | copy-start | bytes 3145732
  (18 other events, 23.1 us)
Sparse Core Ops, SparseCore 0:
  10.1 54.3 all-gather.5
  66.6 60.8 all-gather.3
  319.1 627.7 reduce-scatter.6
  952.3 245.9 reduce-scatter.4
where the time goes:
time: 1210 us
  waiting for transfers between devices  909 us (75%)
  blocking collectives  107 us (9%)
  local copies, waits for them, and re-layouts  69.6 us (6%)
  matrix products  64.6 us (5%)
  other arithmetic  28.5 us (2%)
  between operations  14.6 us (1%)
    unnamed x5, waiting for transfers between devices  543 us
    reduce_scatter x1, waiting for transfers between devices, body(): lax.psum_scatter(grad_qkv, ('ulysses', 'dp'), scatter_dimension=0, tiled=...  251 us
    unnamed x1, blocking collectives  65.3 us
    all_gather x1, waiting for transfers between devices, body(): lax.all_gather(w_qkv, 'dp', axis=0, tiled=True)  59.1 us
    all_gather x1, waiting for transfers between devices, body(): lax.all_gather(w_out, 'dp', axis=0, tiled=True)  35 us
    all_to_all x1, blocking collectives, body(): lax.all_to_all(outgoing, 'ulysses', split_axis=0, concat_axis=1, tiled=True)  24.7 us
  transfers between devices with their start and end apart: 5, of which 5 were waited for; matrix products, arithmetic and copies ran while one was open for 2% of the time, Pallas kernels for 0%

commit v1 on v0

v1 whole, which is shorter than its diff:
```python
import functools
import math

import jax
import jax.numpy as jnp
from jax import lax
from jax.experimental import pallas as pl
from jax.experimental.pallas import tpu as pltpu
from jax.sharding import PartitionSpec as P

HEADS = 16
KV_HEADS = 4
HEAD_DIM = 64
D = 2048
SEQ = 2048
ROWS = 256
QW = 1024
KW = 256
NU = 8
ND = 16
EPS = 1e-05
ROPE_BASE = 500000.0
MESH = pl.DeviceIdType.MESH
F32 = jnp.float32
BF16 = jnp.bfloat16


def doc_positions(doc_lengths, length):
    bounds = jnp.cumsum(doc_lengths) - doc_lengths
    places = jnp.arange(length, dtype=jnp.int32)
    begins = jnp.max(jnp.where(bounds[None, :] <= places[:, None], bounds[None, :], 0), axis=1)
    return begins, places - begins


def rotary_tables_t(places):
    inverse = ROPE_BASE ** (-jnp.arange(0, HEAD_DIM, 2).astype(F32) / HEAD_DIM)
    angles = inverse[:, None] * places.astype(F32)[None, :]
    cos, sin = jnp.cos(angles), jnp.sin(angles)
    return jnp.concatenate([cos, cos], axis=0), jnp.concatenate([sin, sin], axis=0)


def remote(src, dst, send_sem, recv_sem, u, d):
    return pltpu.make_async_remote_copy(
        src_ref=src, dst_ref=dst, send_sem=send_sem, recv_sem=recv_sem,
        device_id={"ulysses": u, "dp": d}, device_id_type=MESH,
    )


def gather_kernel(tok, dout, wqkv, wout, gain, T, G, W, WO, GN,
                  zs, zr, ps, pr, ws, wr, os_, or_, gs, gr, wps, wpr, loc):
    u = lax.axis_index("ulysses")
    d = lax.axis_index("dp")
    z, c = u // 2, u % 2
    right = ((z + 1) % 4) * 2 + c
    left = ((z + 3) % 4) * 2 + c
    far = ((z + 2) % 4) * 2 + c
    mate = z * 2 + (1 - c)

    barrier = pltpu.get_barrier_semaphore()
    for peer in (right, left, mate):
        pl.semaphore_signal(barrier, inc=1, device_id={"ulysses": peer, "dp": d}, device_id_type=MESH)

    @pl.loop(1, ND)
    def _(k):
        pl.semaphore_signal(barrier, inc=1, device_id={"ulysses": u, "dp": (d + k) % ND}, device_id_type=MESH)

    pl.semaphore_wait(barrier, 3 + ND - 1)

    H = ROWS // 2
    A, B = pl.ds(0, H), pl.ds(H, H)
    srcs, dsts = (tok, dout), (T, G)

    def own(a, slot, rows, to):
        return remote(srcs[a].at[rows], dsts[a].at[u, rows], zs.at[a, slot], zr.at[a, slot], to, d)

    def fwd(a, slot, frm, rows, to):
        return remote(dsts[a].at[frm, rows], dsts[a].at[frm, rows], zs.at[a, slot], zr.at[a, slot], to, d)

    def relay(a, slot, frm, rows):
        return remote(dsts[a].at[frm, rows], dsts[a].at[frm, rows], ps.at[a, slot], pr.at[a, slot], mate, d)

    def own_relay(a):
        return remote(srcs[a], dsts[a].at[u], ps.at[a, 6], pr.at[a, 6], mate, d)

    def start_own(a):
        own(a, 0, A, right).start()
        own(a, 3, B, left).start()
        own(a, 1, B, right).start()
        own(a, 2, A, left).start()
        own_relay(a).start()

    start_own(0)

    HW = wqkv.shape[0] // 2

    def w_copy(k):
        to = (d + k) % ND
        return remote(wqkv.at[pl.ds(c * HW, HW)], W.at[d, c], ws.at[k], wr.at[k], u, to)

    def o_copy(k):
        to = (d + k) % ND
        return remote(wout.at[:, pl.ds(pl.multiple_of(u * 128, 128), 128)], WO.at[d], os_.at[k], or_.at[k], u, to)

    def g_copy(k):
        to = (d + k) % ND
        return remote(gain, GN.at[d], gs.at[k], gr.at[k], u, to)

    @pl.loop(1, ND)
    def _(k):
        g_copy(k).start()
        o_copy(k).start()
        w_copy(k).start()

    locals_ = [
        pltpu.make_async_copy(tok, T.at[u], loc.at[0]),
        pltpu.make_async_copy(dout, G.at[u], loc.at[1]),
        pltpu.make_async_copy(wqkv.at[pl.ds(c * HW, HW)], W.at[d, c], loc.at[2]),
        pltpu.make_async_copy(wout.at[:, pl.ds(pl.multiple_of(u * 128, 128), 128)], WO.at[d], loc.at[3]),
        pltpu.make_async_copy(gain, GN.at[d], loc.at[4]),
    ]
    for cp in locals_:
        cp.start()

    def arrivals(a):
        own(a, 0, A, right).wait_recv()
        fwd(a, 4, left, A, right).start()
        relay(a, 0, left, A).start()
        own(a, 3, B, left).wait_recv()
        fwd(a, 5, right, B, left).start()
        relay(a, 3, right, B).start()

    def late(a):
        own(a, 1, B, right).wait_recv()
        relay(a, 1, left, B).start()
        own(a, 2, A, left).wait_recv()
        relay(a, 2, right, A).start()

    def last(a):
        fwd(a, 4, far, A, right).wait_recv()
        relay(a, 4, far, A).start()
        fwd(a, 5, far, B, left).wait_recv()
        relay(a, 5, far, B).start()

    arrivals(0)
    start_own(1)
    late(0)
    last(0)
    arrivals(1)

    for cp in locals_:
        cp.wait()

    @pl.loop(1, ND)
    def _(k):
        g_copy(k).wait()
        o_copy(k).wait()
        w_copy(k).wait()

    w_mate = remote(W.at[:, c], W.at[:, c], wps, wpr, mate, d)
    w_mate.start()
    late(1)
    last(1)
    w_mate.wait()
    for a in range(2):
        own(a, 0, A, right).wait_send()
        own(a, 1, B, right).wait_send()
        own(a, 2, A, left).wait_send()
        own(a, 3, B, left).wait_send()
        fwd(a, 4, left, A, right).wait_send()
        fwd(a, 5, right, B, left).wait_send()
        own_relay(a).wait()
        relay(a, 0, left, A).wait()
        relay(a, 1, left, B).wait()
        relay(a, 2, right, A).wait()
        relay(a, 3, right, B).wait()
        relay(a, 4, far, A).wait()
        relay(a, 5, far, B).wait()


def gather(tok, dout, wqkv, wout, gain):
    dma = pltpu.SemaphoreType.DMA
    hbm = pl.BlockSpec(memory_space=pl.ANY)
    vmem = pl.BlockSpec(memory_space=pltpu.VMEM)
    return pl.pallas_call(
        gather_kernel,
        name="gather",
        out_shape=(
            jax.ShapeDtypeStruct((NU, ROWS, D), BF16),
            jax.ShapeDtypeStruct((NU, ROWS, D), BF16),
            jax.ShapeDtypeStruct((ND, 2, 64, 1536), BF16),
            jax.ShapeDtypeStruct((ND, 128, 128), BF16),
            jax.ShapeDtypeStruct((ND, 8, 128), F32),
        ),
        in_specs=[vmem] * 5,
        out_specs=(hbm,) * 5,
        scratch_shapes=[
            dma((2, 6)), dma((2, 6)), dma((2, 7)), dma((2, 7)),
            dma((ND,)), dma((ND,)), dma((ND,)), dma((ND,)), dma((ND,)), dma((ND,)),
            dma, dma, dma((5,)),
        ],
        compiler_params=pltpu.CompilerParams(collective_id=0, has_side_effects=True),
    )(tok, dout, wqkv, wout, gain)


def rot_t(u, cos, sin):
    half = HEAD_DIM // 2
    return u * cos + jnp.concatenate([-u[half:], u[:half]], axis=0) * sin


def proj_kernel(tok, dout, wsel, wo, gain, cos, sin, normed, q_t, kv_t, kv, da_t):
    wide = tok[0].astype(F32)
    inv = lax.rsqrt(jnp.mean(wide * wide, axis=1, keepdims=True) + EPS)
    low = (wide * inv * gain[...]).astype(BF16)
    normed[...] = low
    proj_t = jnp.dot(low, wsel[...], preferred_element_type=F32).T
    cos_, sin_ = cos[...], sin[...]
    q_t[0:64, :] = rot_t(proj_t[0:64], cos_, sin_).astype(BF16)
    q_t[64:128, :] = rot_t(proj_t[64:128], cos_, sin_).astype(BF16)
    both = jnp.concatenate([rot_t(proj_t[128:192], cos_, sin_), proj_t[192:256]], axis=0)
    kv_t[...] = both.astype(BF16)
    kv[...] = both.T.astype(BF16)
    da_t[...] = jnp.dot(dout[0], wo[...], preferred_element_type=F32).T.astype(BF16)


def project(T, G, wsel, wo, gain, cos_t, sin_t):
    n = SEQ // ROWS
    col = pl.BlockSpec((128, ROWS), lambda i: (0, i))
    fixed = lambda shape: pl.BlockSpec(shape, lambda i: (0, 0))
    return pl.pallas_call(
        proj_kernel,
        name="project",
        grid=(n,),
        in_specs=[
            pl.BlockSpec((1, ROWS, D), lambda i: (i, 0, 0)),
            pl.BlockSpec((1, ROWS, D), lambda i: (i, 0, 0)),
            fixed((D, 256)), fixed((D, 128)), fixed((1, D)),
            pl.BlockSpec((64, ROWS), lambda i: (0, i)),
            pl.BlockSpec((64, ROWS), lambda i: (0, i)),
        ],
        out_specs=(
            pl.BlockSpec((ROWS, D), lambda i: (i, 0)),
            col, col, pl.BlockSpec((ROWS, 128), lambda i: (i, 0)), col,
        ),
        out_shape=(
            jax.ShapeDtypeStruct((SEQ, D), BF16),
            jax.ShapeDtypeStruct((128, SEQ), BF16),
            jax.ShapeDtypeStruct((128, SEQ), BF16),
            jax.ShapeDtypeStruct((SEQ, 128), BF16),
            jax.ShapeDtypeStruct((128, SEQ), BF16),
        ),
    )(T, G, wsel, wo, gain, cos_t, sin_t)


QB = 128
WIN = 512


def attend_kernel(q_t, da_t, begins, cos, sin, kv, kv_t, cos_all, sin_all, attn_t, dq_t, dkv_t, acc):
    i = pl.program_id(0)

    @pl.when(i == 0)
    def _():
        acc[...] = jnp.zeros_like(acc)

    start = pl.multiple_of(jnp.maximum(i - 3, 0) * QB, QB)
    keys = kv[pl.ds(start, WIN), :]
    keys_t = kv_t[:, pl.ds(start, WIN)]
    q = (q_t[...].astype(F32) * (HEAD_DIM ** -0.5)).astype(BF16)
    da = da_t[...]
    none = jnp.zeros((64, 2 * QB), BF16)
    q2 = jnp.concatenate([q[0:64], q[64:128]], axis=1)
    da2 = jnp.concatenate([da[0:64], da[64:128]], axis=1)
    mixed = jnp.concatenate(
        [jnp.concatenate([q2, none], axis=1), jnp.concatenate([none, da2], axis=1)], axis=0
    )
    st = jnp.dot(keys, mixed, preferred_element_type=F32)
    key_pos = start + lax.broadcasted_iota(jnp.int32, (WIN, QB), 0)
    query_pos = i * QB + lax.broadcasted_iota(jnp.int32, (WIN, QB), 1)
    allowed = (key_pos >= begins[...]) & (key_pos <= query_pos)
    s = jnp.concatenate(
        [jnp.where(allowed, st[:, 0:QB], -1e30), jnp.where(allowed, st[:, QB : 2 * QB], -1e30)], axis=1
    )
    w = jnp.exp(s - jnp.max(s, axis=0, keepdims=True))
    p = w * (1.0 / jnp.sum(w, axis=0, keepdims=True))
    pb = p.astype(BF16)
    o = jnp.dot(keys_t, pb, preferred_element_type=F32)[64:128]
    delta = jnp.sum(da2.astype(F32) * o, axis=0, keepdims=True)
    ds = (p * (st[:, 2 * QB :] - delta)).astype(BF16)
    dq = jnp.dot(keys_t, ds, preferred_element_type=F32)[0:64] * (HEAD_DIM ** -0.5)
    attn_t[0:64, :] = o[:, 0:QB].astype(BF16)
    attn_t[64:128, :] = o[:, QB:].astype(BF16)
    cos_, sin_ = cos[...], -sin[...]
    dq_t[0:64, :] = rot_t(dq[:, 0:QB], cos_, sin_).astype(BF16)
    dq_t[64:128, :] = rot_t(dq[:, QB:], cos_, sin_).astype(BF16)
    acc[pl.ds(start, WIN), :] += lax.dot_general(
        jnp.concatenate([ds, pb], axis=1), mixed, (((1,), (1,)), ((), ())), preferred_element_type=F32
    )

    @pl.when(i == pl.num_programs(0) - 1)
    def _():
        for b in range(SEQ // ROWS):
            cols = slice(b * ROWS, (b + 1) * ROWS)
            t = acc[b * ROWS : (b + 1) * ROWS, :].T
            dkv_t[0:64, cols] = rot_t(t[0:64], cos_all[:, cols], -sin_all[:, cols]).astype(BF16)
            dkv_t[64:128, cols] = t[64:128].astype(BF16)


def attend(q_t, da_t, begins, cos_t, sin_t, kv, kv_t):
    n = SEQ // QB
    col = lambda r: pl.BlockSpec((r, QB), lambda i: (0, i))
    fixed = lambda shape: pl.BlockSpec(shape, lambda i: (0, 0))
    return pl.pallas_call(
        attend_kernel,
        name="attend",
        grid=(n,),
        in_specs=[
            col(128), col(128), col(1), col(64), col(64),
            fixed((SEQ, 128)), fixed((128, SEQ)), fixed((64, SEQ)), fixed((64, SEQ)),
        ],
        out_specs=(col(128), col(128), fixed((128, SEQ))),
        out_shape=(jax.ShapeDtypeStruct((128, SEQ), BF16),) * 3,
        scratch_shapes=[pltpu.VMEM((SEQ, 128), F32)],
    )(q_t, da_t, begins, cos_t, sin_t, kv, kv_t, cos_t, sin_t)


def body(tokens, d_out, lengths, gain, w_qkv, w_out):
    u = lax.axis_index("ulysses")
    factor = 1.0 / math.sqrt(SEQ * ND)
    token_rows, grad_rows = tokens[0], d_out[0]
    gain_rep = jnp.broadcast_to(gain.astype(F32)[None, :], (8, 128))
    T, G, W, WO, GN = gather(token_rows, grad_rows, w_qkv, w_out, gain_rep)
    begins, places = doc_positions(lengths[0], SEQ)
    cos_t, sin_t = rotary_tables_t(places)
    gain_wide = GN[:, 0, :].reshape(1, D)
    w_full = W.reshape(D, QW + 2 * KW)
    kv_head = u // 2
    wsel = jnp.concatenate(
        [
            lax.dynamic_slice_in_dim(w_full, u * 128, 128, axis=1),
            lax.dynamic_slice_in_dim(w_full, QW + kv_head * 64, 64, axis=1),
            lax.dynamic_slice_in_dim(w_full, QW + KW + kv_head * 64, 64, axis=1),
        ],
        axis=1,
    )
    normed, q_t, kv_t, kv, da_t = project(T, G, wsel, WO.reshape(D, 128), gain_wide, cos_t, sin_t)
    attn_t, dq_t, dkv_t = attend(q_t, da_t, begins[None, :], cos_t, sin_t, kv, kv_t)

    other = lax.ppermute(dkv_t, "ulysses", [(i, i ^ 1) for i in range(NU)])
    dkv_t = (dkv_t.astype(F32) + other.astype(F32)).astype(BF16)
    mine_t = lax.dynamic_slice_in_dim(dkv_t, (u % 2) * 64, 64, axis=0)
    cols_t = jnp.concatenate([dq_t, mine_t], axis=0)
    back = cols_t.T.reshape(NU, ROWS, 192)
    back = lax.all_to_all(back, "ulysses", split_axis=0, concat_axis=0, tiled=True)
    dq_rows = back[:, :, :128].transpose(1, 0, 2).reshape(ROWS, QW)
    kv_rows = back[:, :, 128:].reshape(4, 2, ROWS, 64)
    dk_rows = kv_rows[:, 0].transpose(1, 0, 2).reshape(ROWS, KW)
    dv_rows = kv_rows[:, 1].transpose(1, 0, 2).reshape(ROWS, KW)
    d_proj = jnp.concatenate([dq_rows, dk_rows, dv_rows], axis=1)

    dw = jnp.concatenate(
        [
            jnp.einsum("ct,td->cd", cols_t, normed, preferred_element_type=F32),
            jnp.einsum("ct,td->cd", attn_t, G.reshape(SEQ, D), preferred_element_type=F32),
        ],
        axis=0,
    ).T
    dw = dw.reshape(NU, ND, 16, 320).transpose(1, 0, 2, 3).reshape(D, 320)
    dw = lax.psum_scatter(dw, "dp", scatter_dimension=0, tiled=True) * factor
    dw = lax.all_to_all(dw.reshape(NU, 16, 320), "ulysses", split_axis=0, concat_axis=0, tiled=True)
    gq = dw[:, :, 0:128].transpose(1, 0, 2).reshape(16, QW)
    gkv = dw[:, :, 128:192].reshape(4, 2, 16, 64)
    gk = gkv[:, 0].transpose(1, 0, 2).reshape(16, KW)
    gv = gkv[:, 1].transpose(1, 0, 2).reshape(16, KW)
    grad_out = dw[:, :, 192:].transpose(1, 0, 2).reshape(16, QW)
    grad_qkv = jnp.concatenate([gq, gk, gv], axis=1)

    wide = token_rows.astype(F32)
    inv = lax.rsqrt(jnp.mean(wide * wide, axis=1, keepdims=True) + EPS)
    unit = wide * inv
    d_normed = jnp.einsum("tc,dc->td", d_proj, w_full, preferred_element_type=F32)
    grad_gain = jnp.sum(d_normed * unit, axis=0) * factor
    scaled = d_normed * gain_wide
    d_rows = inv * (scaled - unit * jnp.mean(scaled * unit, axis=1, keepdims=True))
    d_tokens = (grad_rows.astype(F32) + d_rows).astype(BF16)
    grad_gain = lax.psum_scatter(grad_gain, ("ulysses", "dp"), scatter_dimension=0, tiled=True)
    return d_tokens[None], grad_qkv, grad_out, grad_gain


def solution(mesh):
    in_specs = (
        P("dp", "ulysses", None),
        P("dp", "ulysses", None),
        P("dp", None),
        P("dp"),
        P("dp", None),
        P("dp", None),
    )
    out_specs = (
        P("dp", "ulysses", None),
        P(("ulysses", "dp"), None),
        P(("ulysses", "dp"), None),
        P(("ulysses", "dp")),
    )
    return jax.shard_map(body, mesh=mesh, in_specs=in_specs, out_specs=out_specs, check_vma=False)
```

time: 1210 us -> 331 us (0.27)
  waiting for transfers between devices: 909 us -> 80 us
  Pallas kernels: 0 us -> 120 us
  local copies, waits for them, and re-layouts: 69.6 us -> 14.4 us
  matrix products: 64.6 us -> 12 us
  blocking collectives: 107 us -> 64.3 us
  other arithmetic: 28.5 us -> 11.1 us
    unnamed x5 -> x1, waiting for transfers between devices: 543 us -> 0.02 us
    reduce_scatter x1, waiting for transfers between devices: 251 us -> 68.1 us  [body(): dw = lax.psum_scatter(dw, 'dp', scatter_dimension=0, tiled=True) * factor]
    pallas_call x0 -> x3, Pallas kernels: none -> 120 us  [the longest x1 84.7 us: gather(): pl.pallas_call(gather_kernel, name='gather', out_shape=(jax.ShapeDtypeStr...]
    all_gather x2 -> x0, waiting for transfers between devices: 94.1 us -> none  [the longest x1 59.1 us: body(): lax.all_gather(w_qkv, 'dp', axis=0, tiled=True)]
    dot_general x29 -> x3, matrix products: 64.6 us -> 12 us  [the longest x1 5.22 us: body(): jnp.einsum('tc,dc->td', d_proj, w_full, preferred_element_type=F32)]
    all_to_all x1 -> x0, blocking collectives: 24.7 us -> none  [body(): lax.all_to_all(outgoing, 'ulysses', split_axis=0, concat_axis=1, tiled=True)]
    all_gather x1 -> x0, blocking collectives: 17.3 us -> none  [body(): lax.all_gather(gain, 'dp', axis=0, tiled=True)]
    unnamed x47 -> x16, local copies, waits for them, and re-layouts: 19.8 us -> 2.91 us
  transfers between devices with their start and end apart: 5 -> 4, of which waited for: 5 -> 2; matrix products, arithmetic and copies ran while one was open for 2% -> 4% of each run, Pallas kernels for 0% -> 0%
where the time goes in v1:
time: 331 us; the launch traced here: 330 us
  Pallas kernels  120 us (36%)
  waiting for transfers between devices  80 us (24%)
  blocking collectives  64.3 us (19%)
  local copies, waits for them, and re-layouts  14.4 us (4%)
  between operations  14.3 us (4%)
  starting transfers between devices  13.4 us (4%)
  matrix products  12 us (4%)
  other arithmetic  11.1 us (3%)
    pallas_call x1, Pallas kernels, gather(): pl.pallas_call(gather_kernel, name='gather', out_shape=(jax.ShapeDtypeStr...  84.7 us
    reduce_scatter x1, waiting for transfers between devices, body(): dw = lax.psum_scatter(dw, 'dp', scatter_dimension=0, tiled=True) * factor  68.1 us
    unnamed x1, blocking collectives  64.3 us
    pallas_call x1, Pallas kernels, attend(): pl.pallas_call(attend_kernel, name='attend', grid=(n,), in_specs=[col(128...  20.4 us
    pallas_call x1, Pallas kernels, project(): pl.pallas_call(proj_kernel, name='project', grid=(n,), in_specs=[pl.Block...  15.4 us
    all_to_all x1, waiting for transfers between devices, body(): lax.all_to_all(back, 'ulysses', split_axis=0, concat_axis=0, tiled=True)  11.9 us
    all_to_all x1, starting transfers between devices, body(): lax.all_to_all(dw.reshape(NU, 16, 320), 'ulysses', split_axis=0, concat_a...  6.77 us
  transfers between devices with their start and end apart: 4, of which 2 were waited for; matrix products, arithmetic and copies ran while one was open for 4% of the time, Pallas kernels for 0%

profile of v1, /device:TPU:1, one launch (start us, length us, event | category | flops | bytes accessed | tf_op | source)
XLA Modules:
  0.0 330.0 jit_solution(5913177105120147616)
XLA Ops:
  8.9 1.3 broadcast_in_dim.10.gain
  10.2 84.7 %gather.1 = (bf16[8,256,2048]{2,1,0:T(8,128)(2,1)}, bf16[8,256,2048]{2,1,0:T(8,128)(2,1)}, bf16[16,2,64,1536]{3,2,1,0:T(8,128)(2,1)}, bf16[16,128,128]{2,1,0:T(8,128)(2,1)}, f32[16,8,128]{2,1,0:T(8,128)}) custom-call(bf16[256,2048]{1,0:T(8,128)(2,1)} %bitcast.72, bf16[256,2048]{1,0:T(8,128)(2,1)} %bitcast.73, bf16[128,1536]{1,0:T(8,128)(2,1)} %wqkv.1, ...), custom_call_target="tpu_custom_call" | custom-call | tf_op jit(solution)/shard_map/gather/pallas_call | solution.py:184
  94.9 1.4 fusion.20
  96.3 1.1 constant_dynamic-slice_fusion.2
  97.4 1.6 constant_dynamic-slice_fusion.1
  100.0 1.1 pad_maximum_fusion.2
  101.1 1.3 pad_maximum_fusion.wsel
  102.4 15.4 %project.1 = (bf16[2048,2048]{1,0:T(8,128)(2,1)}, bf16[128,2048]{1,0:T(8,128)(2,1)}, bf16[128,2048]{1,0:T(8,128)(2,1)}, bf16[2048,128]{1,0:T(8,128)(2,1)}, bf16[128,2048]{1,0:T(8,128)(2,1)}) custom-call(bf16[8,256,2048]{2,1,0:T(8,128)(2,1)} %get-tuple-element.17.tok, bf16[8,256,2048]{2,1,0:T(8,128)(2,1)} %get-tuple-element.18.dout, ...), custom_call_target="tpu_custom_call" | custom-call | tf_op jit(solution)/shard_map/project/pallas_call | solution.py:229
  117.8 20.4 %attend.1 = (bf16[128,2048]{1,0:T(8,128)(2,1)}, bf16[128,2048]{1,0:T(8,128)(2,1)}, bf16[128,2048]{1,0:T(8,128)(2,1)}) custom-call(bf16[128,2048]{1,0:T(8,128)(2,1)} %get-tuple-element.22.q_t, bf16[128,2048]{1,0:T(8,128)(2,1)} %get-tuple-element.23.da_t, s32[1,2048]{1,0:T(1,128)} %bitcast.85, f32[64,2048]{1,0:T(8,128)} %get-tuple-element.45.cos.cos_all, ...), custom_call_target="tpu_custom_call" | custom-call | tf_op jit(solution)/shard_map/attend/pallas_call | solution.py:312
  138.4 4.9 %fusion.21 = f32[128,2048]{1,0:T(8,128)S(1)} fusion(bf16[128,2048]{1,0:T(8,128)(2,1)} %get-tuple-element.29, bf16[2048,2048]{1,0:T(8,128)(2,1)} %bitcast.69), kind=kOutput, calls=%fused_computation.52 | convolution fusion | flops 1073741824 | bytes 9961472 | tf_op jit(solution)/shard_map/ct,td->cd/dot_general | solution.py:363
  143.4 1.2 copy-done.6
  144.6 1.9 fusion.18
  146.5 1.7 maximum_bitcast_fusion
  148.2 2.3 copy.32
  150.5 2.0 copy.33
  152.5 1.0 copy-done.3
  154.6 6.4 %all-to-all-start = ((bf16[8,256,192]{1,2,0:T(8,128)(2,1)}), bf16[8,256,192]{1,2,0:T(8,128)(2,1)S(1)}, u32[]{:S(2)}, u32[]{:S(2)}) async-start(bf16[8,256,192]{1,2,0:T(8,128)(2,1)} %bitcast.66), calls=%async_computation | async-start | bytes 1572864 | tf_op jit(solution)/shard_map/all_to_all | solution.py:353
  161.3 11.9 %all-to-all-done = bf16[8,256,192]{1,2,0:T(8,128)(2,1)S(1)} async-done(((bf16[8,256,192]{1,2,0:T(8,128)(2,1)}), bf16[8,256,192]{1,2,0:T(8,128)(2,1)S(1)}, u32[]{:S(2)}, u32[]{:S(2)}) %all-to-all-start) | async-done | bytes 786464 | tf_op jit(solution)/shard_map/all_to_all | solution.py:353
  173.2 5.2 %fusion.8 = (f32[2048]{0:T(1024)S(1)}, f32[256]{0:T(256)S(1)}, f32[256,2048]{1,0:T(8,128)S(1)}) fusion(f32[256]{0:T(256)S(1)} %add_rsqrt_fusion, bf16[1,256,2048]{2,1,0:T(8,128)(2,1)S(1)} %copy-done, f32[2048]{0:T(1024)S(1)} %bitcast.87, bf16[2048,1536]{1,0:T(8,128)(2,1)} %bitcast.80, bf16[256,256]{0,1:T(8,128)(2,1)S(1)} %bitcast.84, ...), kind=kOutput, calls=%fused_computation.11 | convolution fusion | flops 1616639744 | bytes 10242048 | tf_op jit(solution)/shard_map/tc,dc->td/dot_general | solution.py:380
  178.5 1.7 fusion.10
  180.2 68.1 %reduce-scatter.2.cloned.1.call-done = f32[128,320]{1,0:T(8,128)} async-done(((f32[2048,320]{1,0:T(8,128)}), f32[128,320]{1,0:T(8,128)}) %reduce-scatter.2.cloned.1.call-update) | async-done | bytes 163856 | tf_op jit(solution)/shard_map/reduce_scatter | solution.py:368
  248.3 1.6 broadcast_multiply_fusion
  249.9 6.8 %all-to-all-start.1 = ((f32[8,16,320]{2,1,0:T(8,128)}), f32[8,16,320]{2,1,0:T(8,128)S(1)}, u32[]{:S(2)}, u32[]{:S(2)}) async-start(f32[8,16,320]{2,1,0:T(8,128)} %bitcast.24), calls=%async_computation.2 | async-start | bytes 393216 | tf_op jit(solution)/shard_map/all_to_all | solution.py:369
  256.7 64.3 %all-reduce = f32[2048]{0:T(1024)S(1)} all-reduce(f32[2048]{0:T(1024)S(1)} %broadcast_multiply_fusion.1), channel_id=3, replica_groups=mesh['ulysses'=8,'dp'=16] {'ulysses','dp'}, use_global_device_ids=true, to_apply=%region_6.7.clone | all-reduce | flops 2048 | bytes 16384
  (44 shorter events, 6.6 us)
Async XLA Ops:
  7.2 241.1 %reduce-scatter.2.cloned.1.call-start = ((), (), s32[]{:S(2)}) async-start(), calls=%async_computation.3 | async-start | bytes 3342336 | tf_op jit(solution)/shard_map/reduce_scatter | solution.py:368
  8.9 90.1 %copy-start.5 = (s32[2048]{0:T(1024)}, s32[2048]{0:T(1024)S(1)}, u32[]{:S(2)}) copy-start(s32[2048]{0:T(1024)S(1)} %select_reduce_fusion) | copy-start | bytes 24580
  138.2 5.2 %collective-permute-start = (bf16[128,2048]{1,0:T(8,128)(2,1)}, bf16[128,2048]{1,0:T(8,128)(2,1)S(1)}, u32[]{:S(2)}, u32[]{:S(2)}) collective-permute-start(bf16[128,2048]{1,0:T(8,128)(2,1)} %get-tuple-element.27), channel_id=1, source_target_pairs={{0,16},{16,0},{32,48},{48,32},{64,80},{80,64},{96,112},{112,96},{1... | collective-permute-start | bytes 1572872 | tf_op jit(solution)/shard_map/ppermute | solution.py:348
  138.4 5.0 %copy-start.4 = (bf16[128,2048]{1,0:T(8,128)(2,1)S(1)}, bf16[128,2048]{1,0:T(8,128)(2,1)}, u32[]{:S(2)}) copy-start(bf16[128,2048]{1,0:T(8,128)(2,1)} %get-tuple-element.27) | copy-start | bytes 1572868
  138.4 5.1 %copy-start.2 = (bf16[128,2048]{1,0:T(8,128)(2,1)S(1)}, bf16[128,2048]{1,0:T(8,128)(2,1)}, u32[]{:S(2)}) copy-start(bf16[128,2048]{1,0:T(8,128)(2,1)} %get-tuple-element.26) | copy-start | bytes 1572868
  138.4 6.3 %copy-start.6 = (bf16[2048,2048]{1,0:T(8,128)(2,1)S(1)}, bf16[2048,2048]{1,0:T(8,128)(2,1)}, u32[]{:S(2)}) copy-start(bf16[2048,2048]{1,0:T(8,128)(2,1)} %get-tuple-element.28) | copy-start | bytes 25165828
  152.5 1.0 copy-start.3
  153.6 7.4 %copy-start = (bf16[1,256,2048]{2,1,0:T(8,128)(2,1)S(1)}, bf16[1,256,2048]{2,1,0:T(8,128)(2,1)}, u32[]{:S(2)}) copy-start(bf16[1,256,2048]{2,1,0:T(8,128)(2,1)} %param.6) | copy-start | bytes 3145732
  154.6 18.6 %all-to-all-start = ((bf16[8,256,192]{1,2,0:T(8,128)(2,1)}), bf16[8,256,192]{1,2,0:T(8,128)(2,1)S(1)}, u32[]{:S(2)}, u32[]{:S(2)}) async-start(bf16[8,256,192]{1,2,0:T(8,128)(2,1)} %bitcast.66), calls=%async_computation | async-start | bytes 1572864 | tf_op jit(solution)/shard_map/all_to_all | solution.py:353
  173.2 5.2 %copy-start.1 = (bf16[1,256,2048]{2,1,0:T(8,128)(2,1)S(1)}, bf16[1,256,2048]{2,1,0:T(8,128)(2,1)}, u32[]{:S(2)}) copy-start(bf16[1,256,2048]{2,1,0:T(8,128)(2,1)} %param.7) | copy-start | bytes 3145732
  249.9 71.7 %all-to-all-start.1 = ((f32[8,16,320]{2,1,0:T(8,128)}), f32[8,16,320]{2,1,0:T(8,128)S(1)}, u32[]{:S(2)}, u32[]{:S(2)}) async-start(f32[8,16,320]{2,1,0:T(8,128)} %bitcast.24), calls=%async_computation.2 | async-start | bytes 393216 | tf_op jit(solution)/shard_map/all_to_all | solution.py:369
Sparse Core Ops, SparseCore 0:
  152.7 95.5 reduce-scatter.1

commit v2 on v1

--- a/solution.py
+++ b/solution.py
@@ -255,7 +255,7 @@
 WIN = 512
 
 
-def attend_kernel(q_t, da_t, begins, cos, sin, kv, kv_t, cos_all, sin_all, attn_t, dq_t, dkv_t, acc):
+def attend_kernel(q_t, da_t, begins, cos, sin, kv, kv_t, cos_all, sin_all, attn_t, dq_t, dq_n, dkv, acc):
     i = pl.program_id(0)
 
     @pl.when(i == 0)
@@ -290,8 +290,9 @@
     attn_t[0:64, :] = o[:, 0:QB].astype(BF16)
     attn_t[64:128, :] = o[:, QB:].astype(BF16)
     cos_, sin_ = cos[...], -sin[...]
-    dq_t[0:64, :] = rot_t(dq[:, 0:QB], cos_, sin_).astype(BF16)
-    dq_t[64:128, :] = rot_t(dq[:, QB:], cos_, sin_).astype(BF16)
+    turned = jnp.concatenate([rot_t(dq[:, 0:QB], cos_, sin_), rot_t(dq[:, QB:], cos_, sin_)], axis=0)
+    dq_t[...] = turned.astype(BF16)
+    dq_n[...] = turned.T.astype(BF16)
     acc[pl.ds(start, WIN), :] += lax.dot_general(
         jnp.concatenate([ds, pb], axis=1), mixed, (((1,), (1,)), ((), ())), preferred_element_type=F32
     )
@@ -300,9 +301,9 @@
     def _():
         for b in range(SEQ // ROWS):
             cols = slice(b * ROWS, (b + 1) * ROWS)
-            t = acc[b * ROWS : (b + 1) * ROWS, :].T
-            dkv_t[0:64, cols] = rot_t(t[0:64], cos_all[:, cols], -sin_all[:, cols]).astype(BF16)
-            dkv_t[64:128, cols] = t[64:128].astype(BF16)
+            t = acc[cols, :].T
+            t = jnp.concatenate([rot_t(t[0:64], cos_all[:, cols], -sin_all[:, cols]), t[64:128]], axis=0)
+            dkv[cols, :] = t.T.astype(BF16)
 
 
 def attend(q_t, da_t, begins, cos_t, sin_t, kv, kv_t):
@@ -317,15 +318,332 @@
             col(128), col(128), col(1), col(64), col(64),
             fixed((SEQ, 128)), fixed((128, SEQ)), fixed((64, SEQ)), fixed((64, SEQ)),
         ],
-        out_specs=(col(128), col(128), fixed((128, SEQ))),
-        out_shape=(jax.ShapeDtypeStruct((128, SEQ), BF16),) * 3,
+        out_specs=(col(128), col(128), pl.BlockSpec((QB, 128), lambda i: (i, 0)), fixed((SEQ, 128))),
+        out_shape=(jax.ShapeDtypeStruct((128, SEQ), BF16),) * 2 + (jax.ShapeDtypeStruct((SEQ, 128), BF16),) * 2,
         scratch_shapes=[pltpu.VMEM((SEQ, 128), F32)],
     )(q_t, da_t, begins, cos_t, sin_t, kv, kv_t, cos_t, sin_t)
 
 
+FACTOR = 1.0 / math.sqrt(SEQ * ND)
+HALF = 80
+PART = 40
+
+
+def finish_kernel(dq_t, attn_t, dq, dkv, tok, dout, gain, normed_h, g_h, w_h,
+                  dtok_o, gqkv_o, gout_o, ggain_o,
+                  N, GG, W, DP, RKV, OT, KVS, KVT, R, B1, B2, FIN, FKV, DN, gbuf, GR, gsum, GU,
+                  load, ms, mr, qs, qr, ks, kr, rs, rr, fs, fr, vs, vr, gs, gr, us, ur):
+    u = lax.axis_index("ulysses")
+    d = lax.axis_index("dp")
+    z, c = u // 2, u % 2
+    x, y = d // 4, d % 4
+    mate = z * 2 + (1 - c)
+
+    def n_load(f):
+        cols = pl.ds(pl.multiple_of(f * 256, 256), 256)
+        return pltpu.make_async_copy(normed_h.at[:, cols], N.at[f], load.at[0, f])
+
+    def g_load(f):
+        cols = pl.ds(pl.multiple_of(f * 256, 256), 256)
+        return pltpu.make_async_copy(g_h.at[:, cols], GG.at[f], load.at[1, f])
+
+    w_load = pltpu.make_async_copy(w_h, W, load.at[2, 0])
+
+    @pl.loop(0, NU)
+    def _(f):
+        n_load(f).start()
+        g_load(f).start()
+
+    w_load.start()
+
+    barrier = pltpu.get_barrier_semaphore()
+
+    @pl.loop(1, NU)
+    def _(k):
+        pl.semaphore_signal(barrier, inc=1, device_id={"ulysses": (u + k) % NU, "dp": d}, device_id_type=MESH)
+
+    @pl.loop(1, ND)
+    def _(k):
+        pl.semaphore_signal(barrier, inc=1, device_id={"ulysses": u, "dp": (d + k) % ND}, device_id_type=MESH)
+
+    pl.semaphore_wait(barrier, NU + ND - 2)
+
+    def q_copy(k):
+        to = (u + k) % NU
+        rows = pl.ds(pl.multiple_of(to * ROWS, ROWS), ROWS)
+        cols = pl.ds(pl.multiple_of(u * 128, 128), 128)
+        return remote(dq.at[rows], DP.at[:, cols], qs.at[k], qr.at[k], to, d)
+
+    def kv_copy(k):
+        to = (u + k) % NU
+        rows = pl.ds(pl.multiple_of(to * ROWS + c * 128, 128), 128)
+        return remote(KVS.at[rows], RKV.at[z, pl.ds(pl.multiple_of(c * 128, 128), 128)], ks.at[k], kr.at[k], to, d)
+
+    m_copy = remote(dkv, OT, ms, mr, mate, d)
+    m_copy.start()
+
+    @pl.loop(1, NU)
+    def _(k):
+        q_copy(k).start()
+
+    DP[:, pl.ds(pl.multiple_of(u * 128, 128), 128)] = dq[pl.ds(pl.multiple_of(u * ROWS, ROWS), ROWS), :]
+
+    def dw_block(f):
+        n_load(f).wait()
+        g_load(f).wait()
+        rows = pl.ds(pl.multiple_of(f * 16, 16), 16)
+        q = jnp.dot(dq_t[...], N[f], preferred_element_type=F32)
+        R[:, :, rows, 0:128] = q.T.reshape(4, 4, 16, 128)
+        o = jnp.dot(attn_t[...], GG[f], preferred_element_type=F32)
+        R[:, :, rows, 128:256] = o.T.reshape(4, 4, 16, 128)
+
+    dw_block(0)
+
+    m_copy.wait()
+
+    @pl.loop(0, NU)
+    def _(b):
+        rows = pl.ds(pl.multiple_of(b * ROWS, ROWS), ROWS)
+        both = (dkv[rows, :].astype(F32) + OT[rows, :].astype(F32)).astype(BF16)
+        KVS[rows, :] = both
+        KVT[:, rows] = both.astype(F32).T.astype(BF16)
+
+    @pl.loop(1, NU)
+    def _(k):
+        kv_copy(k).start()
+
+    RKV[z, pl.ds(pl.multiple_of(c * 128, 128), 128), :] = KVS[
+        pl.ds(pl.multiple_of(u * ROWS + c * 128, 128), 128), :
+    ]
+
+    @pl.loop(1, 5)
+    def _(f):
+        dw_block(f)
+
+    def along_x(h, st):
+        return (h == 0) == (st == 0)
+
+    def near(h, st, step):
+        if along_x(h, st):
+            return ((x + step) % 4) * 4 + y
+        return x * 4 + (y + step) % 4
+
+    def piece(h, st, step, part):
+        rows = pl.ds(h * HALF + part * PART, PART)
+        if along_x(h, st):
+            j = (x + step) % 4
+            return R.at[j, :, rows, :] if st == 0 else R.at[j, y, rows, :]
+        j = (y + step) % 4
+        return R.at[:, j, rows, :] if st == 0 else R.at[x, j, rows, :]
+
+    def buf(h, st, slot):
+        return B1.at[h, slot] if st == 0 else B2.at[h, slot]
+
+    ROUTE = ((2, 0, 1), (2, 1, 3), (1, 1, 1), (3, 0, 3), (1, 0, 1), (3, 1, 3))
+
+    def rcp(h, st, slot):
+        step, part, to = ROUTE[slot]
+        return remote(piece(h, st, step, part), buf(h, st, slot), rs.at[h, st, slot], rr.at[h, st, slot],
+                      u, near(h, st, to))
+
+    def start(h, st):
+        for slot in range(4):
+            rcp(h, st, slot).start()
+
+    def pass_on(h, st):
+        for slot, step, part in ((0, 1, 0), (1, 3, 1)):
+            rcp(h, st, slot).wait_recv()
+            p = piece(h, st, step, part)
+            p[...] = p[...] + buf(h, st, slot)[...]
+            rcp(h, st, slot + 4).start()
+
+    def gather_up(h, st):
+        for part, one, two in ((0, 3, 4), (1, 2, 5)):
+            rcp(h, st, one).wait_recv()
+            rcp(h, st, two).wait_recv()
+            p = piece(h, st, 0, part)
+            p[...] = p[...] + (buf(h, st, one)[...] + buf(h, st, two)[...])
+
+    start(0, 0)
+
+    @pl.loop(5, NU)
+    def _(f):
+        dw_block(f)
+
+    for i in range(4):
+        kvp = jnp.dot(KVT[...], N[c * 4 + i], preferred_element_type=F32)
+        R[:, :, 128 + (i // 2) * 16 : 144 + (i // 2) * 16, (i % 2) * 128 : (i % 2) * 128 + 128] = (
+            kvp.T.reshape(4, 4, 16, 128)
+        )
+
+    start(1, 0)
+    pass_on(0, 0)
+    pass_on(1, 0)
+
+    @pl.loop(1, NU)
+    def _(k):
+        q_copy(k).wait()
+        kv_copy(k).wait()
+
+    w_load.wait()
+    for i in range(2):
+        a, b = RKV[2 * i], RKV[2 * i + 1]
+        DP[:, QW + i * 128 : QW + (i + 1) * 128] = jnp.concatenate([a[:, 0:64], b[:, 0:64]], axis=1)
+        DP[:, QW + KW + i * 128 : QW + KW + (i + 1) * 128] = jnp.concatenate([a[:, 64:], b[:, 64:]], axis=1)
+
+    wide = tok[...].astype(F32)
+    inv = lax.rsqrt(jnp.mean(wide * wide, axis=1, keepdims=True) + EPS)
+
+    def back(f, along):
+        cols = pl.ds(pl.multiple_of(f * 256, 256), 256)
+        dn = lax.dot_general(DP[...], W[cols, :], (((1,), (1,)), ((), ())), preferred_element_type=F32)
+        unit = tok[:, cols].astype(F32) * inv
+        gbuf[pl.ds(f, 1), :] = jnp.sum(dn * unit, axis=0, keepdims=True)
+        scaled = dn * gain[:, cols]
+        DN[f] = scaled
+        return along + jnp.sum(scaled * unit, axis=1, keepdims=True)
+
+    along = lax.fori_loop(0, NU, back, jnp.zeros((ROWS, 1), F32))
+    mean = along * (1.0 / D)
+
+    def g_copy(k):
+        return remote(gbuf, GR.at[d], gs.at[k], gr.at[k], u, (d + k) % ND)
+
+    @pl.loop(1, ND)
+    def _(k):
+        g_copy(k).start()
+
+    GR[d] = gbuf[...]
+
+    gather_up(0, 0)
+    start(0, 1)
+    gather_up(1, 0)
+    start(1, 1)
+
+    @pl.loop(0, NU)
+    def _(f):
+        cols = pl.ds(pl.multiple_of(f * 256, 256), 256)
+        unit = tok[:, cols].astype(F32) * inv
+        d_rows = inv * (DN[f] - unit * mean)
+        dtok_o[:, cols] = (dout[:, cols].astype(F32) + d_rows).astype(BF16)
+
+    pass_on(0, 1)
+    pass_on(1, 1)
+
+    @pl.loop(1, ND)
+    def _(k):
+        g_copy(k).wait()
+
+    gsum[...] = jnp.sum(GR[...], axis=0)
+
+    def gu_copy(k):
+        return remote(gsum, GU.at[u], us.at[k], ur.at[k], (u + k) % NU, d)
+
+    @pl.loop(1, NU)
+    def _(k):
+        gu_copy(k).start()
+
+    GU[u] = gsum[...]
+    gather_up(0, 1)
+    gather_up(1, 1)
+
+    def f_copy(k):
+        to = (u + k) % NU
+        return remote(R.at[x, y, pl.ds(pl.multiple_of(to * 16, 16), 16)], FIN.at[u], fs.at[k], fr.at[k], to, d)
+
+    @pl.loop(1, NU)
+    def _(k):
+        f_copy(k).start()
+
+    def v_block(i):
+        return R.at[x, y, pl.ds(128 + (i // 2) * 16, 16), pl.ds((i % 2) * 128, 128)]
+
+    def v_copy(i):
+        return remote(v_block(i), FKV.at[z], vs.at[i], vr.at[z], c * 4 + i, d)
+
+    def v_arrival(zs):
+        return remote(v_block(0), FKV.at[zs], vs.at[0], vr.at[zs], u, d)
+
+    for i in range(4):
+        @pl.when(c * 4 + i != u)
+        def _():
+            v_copy(i).start()
+
+        @pl.when(c * 4 + i == u)
+        def _():
+            FKV[z] = v_block(i)[...]
+
+    FIN[u] = R[x, y, pl.ds(pl.multiple_of(u * 16, 16), 16), :]
+
+    @pl.loop(1, NU)
+    def _(k):
+        gu_copy(k).wait()
+
+    ggain_o[...] = jnp.sum(GU[...], axis=0) * FACTOR
+
+    @pl.loop(1, NU)
+    def _(k):
+        f_copy(k).wait()
+
+    for i in range(4):
+        @pl.when(i * 2 + u // 4 != u)
+        def _():
+            v_arrival(i).wait_recv()
+
+        @pl.when(c * 4 + i != u)
+        def _():
+            v_copy(i).wait_send()
+
+    for i in range(NU):
+        gqkv_o[:, i * 128 : (i + 1) * 128] = FIN[i, :, 0:128] * FACTOR
+        gout_o[:, i * 128 : (i + 1) * 128] = FIN[i, :, 128:256] * FACTOR
+    for i in range(2):
+        a, b = FKV[2 * i] * FACTOR, FKV[2 * i + 1] * FACTOR
+        gqkv_o[:, QW + i * 128 : QW + (i + 1) * 128] = jnp.concatenate([a[:, 0:64], b[:, 0:64]], axis=1)
+        gqkv_o[:, QW + KW + i * 128 : QW + KW + (i + 1) * 128] = jnp.concatenate([a[:, 64:], b[:, 64:]], axis=1)
+
+    for h in range(2):
+        for st in range(2):
+            for slot in range(6):
+                rcp(h, st, slot).wait_send()
+
+
+def finish(dq_t, attn_t, dq, dkv, tok, dout, gain, normed, g, w):
+    dma = pltpu.SemaphoreType.DMA
+    hbm = pl.BlockSpec(memory_space=pl.ANY)
+    vmem = pl.BlockSpec(memory_space=pltpu.VMEM)
+    V = pltpu.VMEM
+    return pl.pallas_call(
+        finish_kernel,
+        name="finish",
+        out_shape=(
+            jax.ShapeDtypeStruct((ROWS, D), BF16),
+            jax.ShapeDtypeStruct((16, QW + 2 * KW), F32),
+            jax.ShapeDtypeStruct((16, QW), F32),
+            jax.ShapeDtypeStruct((NU, 256), F32),
+        ),
+        in_specs=[vmem] * 7 + [hbm] * 3,
+        out_specs=(vmem,) * 4,
+        scratch_shapes=[
+            V((NU, SEQ, 256), BF16), V((NU, SEQ, 256), BF16), V((D, QW + 2 * KW), BF16),
+            V((ROWS, QW + 2 * KW), BF16), V((4, ROWS, 128), BF16),
+            V((SEQ, 128), BF16), V((SEQ, 128), BF16), V((128, SEQ), BF16),
+            V((4, 4, 2 * HALF, 256), F32), V((2, 6, 4, PART, 256), F32), V((2, 6, PART, 256), F32),
+            V((NU, 16, 256), F32), V((4, 16, 128), F32), V((NU, ROWS, 256), F32),
+            V((NU, 256), F32), V((ND, NU, 256), F32), V((NU, 256), F32), V((NU, NU, 256), F32),
+            dma((3, NU)), dma, dma, dma((NU,)), dma((NU,)), dma((NU,)), dma((NU,)),
+            dma((2, 2, 6)), dma((2, 2, 6)), dma((NU,)), dma((NU,)), dma((4,)), dma((4,)),
+            dma((ND,)), dma((ND,)), dma((NU,)), dma((NU,)),
+        ],
+        compiler_params=pltpu.CompilerParams(
+            collective_id=1, has_side_effects=True, vmem_limit_bytes=60 * 1024 * 1024
+        ),
+    )(dq_t, attn_t, dq, dkv, tok, dout, gain, normed, g, w)
+
+
 def body(tokens, d_out, lengths, gain, w_qkv, w_out):
     u = lax.axis_index("ulysses")
-    factor = 1.0 / math.sqrt(SEQ * ND)
+    d = lax.axis_index("dp")
     token_rows, grad_rows = tokens[0], d_out[0]
     gain_rep = jnp.broadcast_to(gain.astype(F32)[None, :], (8, 128))
     T, G, W, WO, GN = gather(token_rows, grad_rows, w_qkv, w_out, gain_rep)
@@ -343,46 +661,11 @@
         axis=1,
     )
     normed, q_t, kv_t, kv, da_t = project(T, G, wsel, WO.reshape(D, 128), gain_wide, cos_t, sin_t)
-    attn_t, dq_t, dkv_t = attend(q_t, da_t, begins[None, :], cos_t, sin_t, kv, kv_t)
-
-    other = lax.ppermute(dkv_t, "ulysses", [(i, i ^ 1) for i in range(NU)])
-    dkv_t = (dkv_t.astype(F32) + other.astype(F32)).astype(BF16)
-    mine_t = lax.dynamic_slice_in_dim(dkv_t, (u % 2) * 64, 64, axis=0)
-    cols_t = jnp.concatenate([dq_t, mine_t], axis=0)
-    back = cols_t.T.reshape(NU, ROWS, 192)
-    back = lax.all_to_all(back, "ulysses", split_axis=0, concat_axis=0, tiled=True)
-    dq_rows = back[:, :, :128].transpose(1, 0, 2).reshape(ROWS, QW)
-    kv_rows = back[:, :, 128:].reshape(4, 2, ROWS, 64)
-    dk_rows = kv_rows[:, 0].transpose(1, 0, 2).reshape(ROWS, KW)
-    dv_rows = kv_rows[:, 1].transpose(1, 0, 2).reshape(ROWS, KW)
-    d_proj = jnp.concatenate([dq_rows, dk_rows, dv_rows], axis=1)
-
-    dw = jnp.concatenate(
-        [
-            jnp.einsum("ct,td->cd", cols_t, normed, preferred_element_type=F32),
-            jnp.einsum("ct,td->cd", attn_t, G.reshape(SEQ, D), preferred_element_type=F32),
-        ],
-        axis=0,
-    ).T
-    dw = dw.reshape(NU, ND, 16, 320).transpose(1, 0, 2, 3).reshape(D, 320)
-    dw = lax.psum_scatter(dw, "dp", scatter_dimension=0, tiled=True) * factor
-    dw = lax.all_to_all(dw.reshape(NU, 16, 320), "ulysses", split_axis=0, concat_axis=0, tiled=True)
-    gq = dw[:, :, 0:128].transpose(1, 0, 2).reshape(16, QW)
-    gkv = dw[:, :, 128:192].reshape(4, 2, 16, 64)
-    gk = gkv[:, 0].transpose(1, 0, 2).reshape(16, KW)
-    gv = gkv[:, 1].transpose(1, 0, 2).reshape(16, KW)
-    grad_out = dw[:, :, 192:].transpose(1, 0, 2).reshape(16, QW)
-    grad_qkv = jnp.concatenate([gq, gk, gv], axis=1)
-
-    wide = token_rows.astype(F32)
-    inv = lax.rsqrt(jnp.mean(wide * wide, axis=1, keepdims=True) + EPS)
-    unit = wide * inv
-    d_normed = jnp.einsum("tc,dc->td", d_proj, w_full, preferred_element_type=F32)
-    grad_gain = jnp.sum(d_normed * unit, axis=0) * factor
-    scaled = d_normed * gain_wide
-    d_rows = inv * (scaled - unit * jnp.mean(scaled * unit, axis=1, keepdims=True))
-    d_tokens = (grad_rows.astype(F32) + d_rows).astype(BF16)
-    grad_gain = lax.psum_scatter(grad_gain, ("ulysses", "dp"), scatter_dimension=0, tiled=True)
+    attn_t, dq_t, dq, dkv = attend(q_t, da_t, begins[None, :], cos_t, sin_t, kv, kv_t)
+    d_tokens, grad_qkv, grad_out, gain_sum = finish(
+        dq_t, attn_t, dq, dkv, token_rows, grad_rows, gain_wide, normed, G.reshape(SEQ, D), w_full
+    )
+    grad_gain = lax.dynamic_slice(gain_sum, (u, d * 16), (1, 16)).reshape(16)
     return d_tokens[None], grad_qkv, grad_out, grad_gain
 
 

time: 331 us -> 204 us (0.62)
  waiting for transfers between devices: 80 us -> 0 us
  Pallas kernels: 120 us -> 185 us
  blocking collectives: 64.3 us -> 0 us
  between operations: 14.3 us -> 0.71 us
  starting transfers between devices: 13.4 us -> 0 us
  matrix products: 12 us -> 0 us
  other arithmetic: 11.1 us -> 5.03 us
    reduce_scatter x1 -> x0, waiting for transfers between devices: 68.1 us -> none  [body(): dw = lax.psum_scatter(dw, 'dp', scatter_dimension=0, tiled=True) * factor]
    pallas_call x0 -> x1, Pallas kernels: none -> 64.4 us  [finish(): pl.pallas_call(finish_kernel, name='finish', out_shape=(jax.ShapeDtypeStr...]
    unnamed x1 -> x0, blocking collectives: 64.3 us -> none
    all_to_all x2 -> x0, starting transfers between devices: 13.2 us -> none  [the longest x1 6.77 us: body(): lax.all_to_all(dw.reshape(NU, 16, 320), 'ulysses', split_axis=0, concat_a...]
    dot_general x3 -> x0, matrix products: 12 us -> none  [the longest x1 5.22 us: body(): jnp.einsum('tc,dc->td', d_proj, w_full, preferred_element_type=F32)]
    all_to_all x2 -> x0, waiting for transfers between devices: 11.9 us -> none  [the longest x1 11.9 us: body(): lax.all_to_all(back, 'ulysses', split_axis=0, concat_axis=0, tiled=True)]
    transpose x5 -> x0, local copies, waits for them, and re-layouts: 4.32 us -> none  [the longest x1 2.28 us: body(): dw = jnp.concatenate([jnp.einsum('ct,td->cd', cols_t, normed, preferred_e...]
  transfers between devices with their start and end apart: 4 -> 0, of which waited for: 2 -> 0; matrix products, arithmetic and copies ran while one was open for 4% -> 0% of each run, Pallas kernels for 0% -> 0%
where the time goes in v2:
time: 204 us; the launch traced here: 203 us
  Pallas kernels  185 us (91%)
  local copies, waits for them, and re-layouts  12 us (6%)
  other arithmetic  5.03 us (2%)
    pallas_call x1, Pallas kernels, gather(): pl.pallas_call(gather_kernel, name='gather', out_shape=(jax.ShapeDtypeStr...  84.7 us
    pallas_call x1, Pallas kernels, finish(): pl.pallas_call(finish_kernel, name='finish', out_shape=(jax.ShapeDtypeStr...  64.4 us
    pallas_call x1, Pallas kernels, attend(): pl.pallas_call(attend_kernel, name='attend', grid=(n,), in_specs=[col(128...  20.9 us
    pallas_call x1, Pallas kernels, project(): pl.pallas_call(proj_kernel, name='project', grid=(n,), in_specs=[pl.Block...  15.5 us
    unnamed x5, local copies, waits for them, and re-layouts  5.32 us

profile of v2, /device:TPU:1, one launch (start us, length us, event | category | flops | bytes accessed | tf_op | source)
XLA Modules:
  0.0 203.2 jit_solution(15982650692617107681)
XLA Ops:
  0.7 0.8 reduce-window_clone.1
  1.5 0.7 subtract_bitcast_fusion
  2.2 1.3 broadcast_in_dim.10.gain
  3.4 0.1 select_reduce_fusion
  3.5 0.0 copy-start
  3.6 1.0 multiply_sine_fusion
  4.6 1.1 pad_maximum_fusion.1
  5.7 84.7 %gather.1 = (bf16[8,256,2048]{2,1,0:T(8,128)(2,1)}, bf16[8,256,2048]{2,1,0:T(8,128)(2,1)}, bf16[16,2,64,1536]{3,2,1,0:T(8,128)(2,1)}, bf16[16,128,128]{2,1,0:T(8,128)(2,1)}, f32[16,8,128]{2,1,0:T(8,128)}) custom-call(bf16[256,2048]{1,0:T(8,128)(2,1)} %bitcast.17, bf16[256,2048]{1,0:T(8,128)(2,1)} %bitcast.19, bf16[128,1536]{1,0:T(8,128)(2,1)} %wqkv.1, ...), custom_call_target="tpu_custom_call" | custom-call | tf_op jit(solution)/shard_map/gather/pallas_call | solution.py:184
  90.4 1.4 slice_bitcast_fusion.gain
  91.8 1.1 constant_dynamic-slice_fusion.2
  92.9 1.6 constant_dynamic-slice_fusion.1
  94.5 1.3 pad_maximum_fusion.wsel
  95.8 15.5 %project.1 = (bf16[2048,2048]{1,0:T(8,128)(2,1)}, bf16[128,2048]{1,0:T(8,128)(2,1)}, bf16[128,2048]{1,0:T(8,128)(2,1)}, bf16[2048,128]{1,0:T(8,128)(2,1)}, bf16[128,2048]{1,0:T(8,128)(2,1)}) custom-call(bf16[8,256,2048]{2,1,0:T(8,128)(2,1)} %get-tuple-element.22.tok, bf16[8,256,2048]{2,1,0:T(8,128)(2,1)} %get-tuple-element.23.dout, ...), custom_call_target="tpu_custom_call" | custom-call | tf_op jit(solution)/shard_map/project/pallas_call | solution.py:229
  111.2 0.0 copy-done
  111.2 20.9 %attend.1 = (bf16[128,2048]{1,0:T(8,128)(2,1)}, bf16[128,2048]{1,0:T(8,128)(2,1)}, bf16[2048,128]{1,0:T(8,128)(2,1)}, bf16[2048,128]{1,0:T(8,128)(2,1)}) custom-call(bf16[128,2048]{1,0:T(8,128)(2,1)} %get-tuple-element.27.q_t, bf16[128,2048]{1,0:T(8,128)(2,1)} %get-tuple-element.28.da_t, s32[1,2048]{1,0:T(1,128)} %bitcast.23, ...), custom_call_target="tpu_custom_call" | custom-call | tf_op jit(solution)/shard_map/attend/pallas_call | solution.py:313
  132.2 64.4 %finish.1 = (bf16[256,2048]{1,0:T(8,128)(2,1)}, f32[16,1536]{1,0:T(8,128)}, f32[16,1024]{1,0:T(8,128)}, f32[8,256]{1,0:T(8,128)}) custom-call(bf16[128,2048]{1,0:T(8,128)(2,1)} %get-tuple-element.31.dq_t, bf16[128,2048]{1,0:T(8,128)(2,1)} %get-tuple-element.32.attn_t, bf16[2048,128]{1,0:T(8,128)(2,1)} %get-tuple-element.33.dq, ...), custom_call_target="tpu_custom_call" | custom-call | tf_op jit(solution)/shard_map/finish/pallas_call | solution.py:616
  196.6 1.3 dynamic-slice_bitcast_fusion
  197.9 2.3 %copy.13 = bf16[1,256,2048]{2,1,0:T(8,128)(2,1)} copy(bf16[1,256,2048]{2,1,0:T(8,128)(2,1)} %bitcast.21) | data formatting | bytes 2097152
  200.2 1.5 copy.14
  201.7 1.5 copy.15
  (2 shorter events, 0.0 us)
Async XLA Ops:
  3.5 107.7 %copy-start = (s32[2048]{0:T(1024)}, s32[2048]{0:T(1024)S(1)}, u32[]{:S(2)}) copy-start(s32[2048]{0:T(1024)S(1)} %select_reduce_fusion) | copy-start | bytes 24580

commit v3 on v2

v3 whole, which is shorter than its diff:
```python
import math

import jax
import jax.numpy as jnp
from jax import lax
from jax.experimental import pallas as pl
from jax.experimental.pallas import tpu as pltpu
from jax.sharding import PartitionSpec as P

HEADS = 16
KV_HEADS = 4
HEAD_DIM = 64
D = 2048
SEQ = 2048
ROWS = 256
QW = 1024
KW = 256
NU = 8
ND = 16
EPS = 1e-05
ROPE_BASE = 500000.0
MESH = pl.DeviceIdType.MESH
F32 = jnp.float32
BF16 = jnp.bfloat16


def doc_positions(doc_lengths, length):
    bounds = jnp.cumsum(doc_lengths) - doc_lengths
    places = jnp.arange(length, dtype=jnp.int32)
    begins = jnp.max(jnp.where(bounds[None, :] <= places[:, None], bounds[None, :], 0), axis=1)
    return begins, places - begins


def rotary_tables_t(places):
    inverse = ROPE_BASE ** (-jnp.arange(0, HEAD_DIM, 2).astype(F32) / HEAD_DIM)
    angles = inverse[:, None] * places.astype(F32)[None, :]
    cos, sin = jnp.cos(angles), jnp.sin(angles)
    return jnp.concatenate([cos, cos], axis=0), jnp.concatenate([sin, sin], axis=0)


def remote(src, dst, send_sem, recv_sem, u, d):
    return pltpu.make_async_remote_copy(
        src_ref=src, dst_ref=dst, send_sem=send_sem, recv_sem=recv_sem,
        device_id={"ulysses": u, "dp": d}, device_id_type=MESH,
    )


QB = 128
WIN = 512
FACTOR = 1.0 / math.sqrt(SEQ * ND)
HALF = 80
PART = 40


def rot_t(u, cos, sin):
    half = HEAD_DIM // 2
    return u * cos + jnp.concatenate([-u[half:], u[:half]], axis=0) * sin


def step_kernel(tok, dout, begins, cos, sin, gain_in, wqkv, wout,
                dtok_o, gqkv_o, gout_o, ggain_o,
                T, N, G, W, WO, GN, gain_rows, gain, WS, q_t, kv_t, kv, da_t, attn_t, dq_t, dq, dkv, acc,
                DP, RKV, OT, KVS, KVT, R, B1, B2, FIN, FKV, DN, gbuf, GR, gsum, GU,
                zs, zr, ps, pr, ws, wr, os_, or_, gns, gnr, wps, wpr, loc,
                ms, mr, qs, qr, ks, kr, rs, rr, fs, fr, vs, vr, gs, gr, us, ur):
    u = lax.axis_index("ulysses")
    d = lax.axis_index("dp")
    z, c = u // 2, u % 2
    x, y = d // 4, d % 4
    right = ((z + 1) % 4) * 2 + c
    left = ((z + 3) % 4) * 2 + c
    far = ((z + 2) % 4) * 2 + c
    mate = z * 2 + (1 - c)

    gain_rows[...] = jnp.broadcast_to(gain_in[...].astype(F32), (8, 128))
    barrier = pltpu.get_barrier_semaphore()

    @pl.loop(1, NU)
    def _(k):
        pl.semaphore_signal(barrier, inc=1, device_id={"ulysses": (u + k) % NU, "dp": d}, device_id_type=MESH)

    @pl.loop(1, ND)
    def _(k):
        pl.semaphore_signal(barrier, inc=1, device_id={"ulysses": u, "dp": (d + k) % ND}, device_id_type=MESH)

    pl.semaphore_wait(barrier, NU + ND - 2)

    H = ROWS // 2
    A, B = pl.ds(0, H), pl.ds(H, H)
    srcs, dsts = (tok, dout), (T, G)

    def own(a, slot, rows, to):
        return remote(srcs[a].at[rows], dsts[a].at[u, rows], zs.at[a, slot], zr.at[a, slot], to, d)

    def fwd(a, slot, frm, rows, to):
        return remote(dsts[a].at[frm, rows], dsts[a].at[frm, rows], zs.at[a, slot], zr.at[a, slot], to, d)

    def relay(a, slot, frm, rows):
        return remote(dsts[a].at[frm, rows], dsts[a].at[frm, rows], ps.at[a, slot], pr.at[a, slot], mate, d)

    def own_relay(a):
        return remote(srcs[a], dsts[a].at[u], ps.at[a, 6], pr.at[a, 6], mate, d)

    def start_own(a):
        own(a, 0, A, right).start()
        own(a, 3, B, left).start()
        own(a, 1, B, right).start()
        own(a, 2, A, left).start()
        own_relay(a).start()

    start_own(0)

    def along_x(h, st):
        return (h == 0) == (st == 0)

    def near(h, st, step):
        if along_x(h, st):
            return ((x + step) % 4) * 4 + y
        return x * 4 + (y + step) % 4

    def w_piece(h, st, step, part):
        rows = pl.ds(h * 32 + part * 16, 16)
        if along_x(h, st):
            j = (x + step) % 4
            return W.at[j, y, c, rows] if st == 0 else W.at[j, :, c, rows]
        j = (y + step) % 4
        return W.at[x, j, c, rows] if st == 0 else W.at[:, j, c, rows]

    W_ROUTE = ((0, 0, 1), (0, 1, 3), (0, 1, 1), (0, 0, 3), (3, 0, 1), (1, 1, 3))

    def w_copy(h, st, slot):
        step, part, to = W_ROUTE[slot]
        if st == 0 and step == 0:
            src = wqkv.at[pl.ds(c * 64 + h * 32 + part * 16, 16)]
        else:
            src = w_piece(h, st, step, part)
        return remote(src, w_piece(h, st, step, part), ws.at[h, st, slot], wr.at[h, st, slot], u, near(h, st, to))

    def w_start(h, st):
        for slot in range(4):
            w_copy(h, st, slot).start()

    def w_pass(h, st):
        for slot in range(2):
            w_copy(h, st, slot).wait_recv()
            w_copy(h, st, slot + 4).start()

    def w_end(h, st):
        for slot in range(2, 6):
            w_copy(h, st, slot).wait_recv()

    def o_copy(k):
        to = (d + k) % ND
        return remote(wout.at[:, pl.ds(pl.multiple_of(u * 128, 128), 128)], WO.at[d], os_.at[k], or_.at[k], u, to)

    def gain_copy(k):
        to = (d + k) % ND
        return remote(gain_rows, GN.at[d], gns.at[k], gnr.at[k], u, to)

    w_local = pltpu.make_async_copy(wqkv.at[pl.ds(c * 64, 64)], W.at[x, y, c], loc)
    w_local.start()
    w_start(0, 0)
    w_start(1, 0)

    @pl.loop(1, ND)
    def _(k):
        gain_copy(k).start()

    T[u] = tok[...]
    G[u] = dout[...]
    GN[d] = gain_rows[...]
    WO[d] = wout[:, pl.ds(pl.multiple_of(u * 128, 128), 128)]

    def arrivals(a):
        own(a, 0, A, right).wait_recv()
        fwd(a, 4, left, A, right).start()
        relay(a, 0, left, A).start()
        own(a, 3, B, left).wait_recv()
        fwd(a, 5, right, B, left).start()
        relay(a, 3, right, B).start()

    def late(a):
        own(a, 1, B, right).wait_recv()
        relay(a, 1, left, B).start()
        own(a, 2, A, left).wait_recv()
        relay(a, 2, right, A).start()

    def last(a):
        fwd(a, 4, far, A, right).wait_recv()
        relay(a, 4, far, A).start()
        fwd(a, 5, far, B, left).wait_recv()
        relay(a, 5, far, B).start()

    def norm(ch):
        @pl.loop(0, ROWS // 32)
        def _(r):
            rows = pl.ds(pl.multiple_of(r * 32, 32), 32)
            wide = T[ch, rows, :].astype(F32)
            inv = lax.rsqrt(jnp.mean(wide * wide, axis=1, keepdims=True) + EPS)
            N[ch, rows, :] = (wide * inv * gain[...]).astype(BF16)

    def chunk_cols(ch):
        return pl.ds(pl.multiple_of(ch * ROWS, ROWS), ROWS)

    def project(ch):
        cols = chunk_cols(ch)
        proj_t = jnp.dot(N[ch], WS[...], preferred_element_type=F32).T
        cos_, sin_ = cos[:, cols], sin[:, cols]
        q_t[0:64, cols] = rot_t(proj_t[0:64], cos_, sin_).astype(BF16)
        q_t[64:128, cols] = rot_t(proj_t[64:128], cos_, sin_).astype(BF16)
        both = jnp.concatenate([rot_t(proj_t[128:192], cos_, sin_), proj_t[192:256]], axis=0)
        kv_t[:, cols] = both.astype(BF16)
        kv[cols, :] = both.T.astype(BF16)

    def attend(ch):
        da_t[:, chunk_cols(ch)] = jnp.dot(
            G[ch], WO[...].reshape(D, 128), preferred_element_type=F32
        ).T.astype(BF16)

        @pl.loop(ch * 2, ch * 2 + 2)
        def _(i):
            attend_block(i)

    def attend_block(i):
        start = pl.multiple_of(jnp.maximum(i - 3, 0) * QB, QB)
        here = pl.ds(pl.multiple_of(i * QB, QB), QB)
        keys = kv[pl.ds(start, WIN), :]
        keys_t = kv_t[:, pl.ds(start, WIN)]
        q = (q_t[:, here].astype(F32) * (HEAD_DIM ** -0.5)).astype(BF16)
        da = da_t[:, here]
        none = jnp.zeros((64, 2 * QB), BF16)
        q2 = jnp.concatenate([q[0:64], q[64:128]], axis=1)
        da2 = jnp.concatenate([da[0:64], da[64:128]], axis=1)
        mixed = jnp.concatenate(
            [jnp.concatenate([q2, none], axis=1), jnp.concatenate([none, da2], axis=1)], axis=0
        )
        st = jnp.dot(keys, mixed, preferred_element_type=F32)
        key_pos = start + lax.broadcasted_iota(jnp.int32, (WIN, QB), 0)
        query_pos = i * QB + lax.broadcasted_iota(jnp.int32, (WIN, QB), 1)
        allowed = (key_pos >= begins[:, here]) & (key_pos <= query_pos)
        s = jnp.concatenate(
            [jnp.where(allowed, st[:, 0:QB], -1e30), jnp.where(allowed, st[:, QB : 2 * QB], -1e30)], axis=1
        )
        w = jnp.exp(s - jnp.max(s, axis=0, keepdims=True))
        p = w * (1.0 / jnp.sum(w, axis=0, keepdims=True))
        pb = p.astype(BF16)
        o = jnp.dot(keys_t, pb, preferred_element_type=F32)[64:128]
        delta = jnp.sum(da2.astype(F32) * o, axis=0, keepdims=True)
        ds = (p * (st[:, 2 * QB :] - delta)).astype(BF16)
        g = jnp.dot(keys_t, ds, preferred_element_type=F32)[0:64] * (HEAD_DIM ** -0.5)
        attn_t[0:64, here] = o[:, 0:QB].astype(BF16)
        attn_t[64:128, here] = o[:, QB:].astype(BF16)
        cos_, sin_ = cos[:, here], -sin[:, here]
        turned = jnp.concatenate([rot_t(g[:, 0:QB], cos_, sin_), rot_t(g[:, QB:], cos_, sin_)], axis=0)
        dq_t[:, here] = turned.astype(BF16)
        dq[here, :] = turned.T.astype(BF16)
        acc[pl.ds(start, WIN), :] += lax.dot_general(
            jnp.concatenate([ds, pb], axis=1), mixed, (((1,), (1,)), ((), ())), preferred_element_type=F32
        )

    acc[...] = jnp.zeros_like(acc)

    w_pass(0, 0)
    w_pass(1, 0)
    w_local.wait()
    for h in range(2):
        w_end(h, 0)
        w_start(h, 1)

    @pl.loop(1, ND)
    def _(k):
        gain_copy(k).wait()
        o_copy(k).start()

    for i in range(ND):
        gain[:, i * 128 : (i + 1) * 128] = GN[i, 0:1, :]
    norm(u)
    arrivals(0)
    start_own(1)
    own_relay(0).wait_recv()
    norm(mate)
    w_pass(0, 1)
    w_pass(1, 1)
    w_end(0, 1)
    w_end(1, 1)
    w_mate = remote(W.at[:, :, c], W.at[:, :, c], wps, wpr, mate, d)
    w_mate.start()
    late(0)

    @pl.loop(0, 2)
    def _(n):
        norm(((z + 1 + 2 * n) % 4) * 2 + c)

    last(0)
    for slot, rows in ((0, A), (1, B), (2, A), (3, B)):
        relay(0, slot, left, rows).wait_recv()

    @pl.loop(0, 3)
    def _(n):
        norm(jnp.where(n == 2, far, ((z + 1 + 2 * n) % 4) * 2 + (1 - c)))

    w_mate.wait()
    WS[:, 0:128] = W[:, :, :, :, pl.ds(pl.multiple_of(u * 128, 128), 128)].reshape(D, 128)
    k_tile = W[:, :, :, :, pl.ds(pl.multiple_of(QW + (z // 2) * 128, 128), 128)].reshape(D, 128)
    v_tile = W[:, :, :, :, pl.ds(pl.multiple_of(QW + KW + (z // 2) * 128, 128), 128)].reshape(D, 128)

    @pl.when(z % 2 == 0)
    def _():
        WS[:, 128:256] = jnp.concatenate([k_tile[:, 0:64], v_tile[:, 0:64]], axis=1)

    @pl.when(z % 2 == 1)
    def _():
        WS[:, 128:256] = jnp.concatenate([k_tile[:, 64:], v_tile[:, 64:]], axis=1)

    relay(0, 4, far, A).wait_recv()
    relay(0, 5, far, B).wait_recv()
    norm(((z + 2) % 4) * 2 + (1 - c))

    @pl.loop(0, NU)
    def _(n):
        project(n)

    @pl.loop(1, ND)
    def _(k):
        o_copy(k).wait()

    arrivals(1)
    own_relay(1).wait_recv()

    @pl.loop(0, 2)
    def _(n):
        attend(z * 2 + n)

    late(1)
    for slot, rows in ((0, A), (1, B), (2, A), (3, B)):
        relay(1, slot, left, rows).wait_recv()

    @pl.loop(0, 4)
    def _(n):
        attend(((z + 1 + 2 * (n // 2)) % 4) * 2 + n % 2)

    last(1)

    @pl.loop(0, 2)
    def _(n):
        @pl.when(n == 1)
        def _():
            relay(1, 4, far, A).wait_recv()
            relay(1, 5, far, B).wait_recv()

        attend(((z + 2) % 4) * 2 + (c + n) % 2)

    @pl.loop(0, NU)
    def _(b):
        cols = chunk_cols(b)
        t = acc[cols, :].T
        t = jnp.concatenate([rot_t(t[0:64], cos[:, cols], -sin[:, cols]), t[64:128]], axis=0)
        dkv[cols, :] = t.T.astype(BF16)

    def q_copy(k):
        to = (u + k) % NU
        rows = pl.ds(pl.multiple_of(to * ROWS, ROWS), ROWS)
        cols = pl.ds(pl.multiple_of(u * 128, 128), 128)
        return remote(dq.at[rows], DP.at[:, cols], qs.at[k], qr.at[k], to, d)

    def kv_copy(k):
        to = (u + k) % NU
        rows = pl.ds(pl.multiple_of(to * ROWS + c * 128, 128), 128)
        return remote(KVS.at[rows], RKV.at[z, pl.ds(pl.multiple_of(c * 128, 128), 128)], ks.at[k], kr.at[k], to, d)

    m_copy = remote(dkv, OT, ms, mr, mate, d)
    m_copy.start()

    @pl.loop(1, NU)
    def _(k):
        q_copy(k).start()

    DP[:, pl.ds(pl.multiple_of(u * 128, 128), 128)] = dq[pl.ds(pl.multiple_of(u * ROWS, ROWS), ROWS), :]

    def dw_block(f):
        cols = pl.ds(pl.multiple_of(f * 256, 256), 256)
        rows = pl.ds(pl.multiple_of(f * 16, 16), 16)
        q = jnp.dot(dq_t[...], N[:, :, cols].reshape(SEQ, 256), preferred_element_type=F32)
        R[:, :, rows, 0:128] = q.T.reshape(4, 4, 16, 128)
        o = jnp.dot(attn_t[...], G[:, :, cols].reshape(SEQ, 256), preferred_element_type=F32)
        R[:, :, rows, 128:256] = o.T.reshape(4, 4, 16, 128)

    dw_block(0)

    m_copy.wait()

    @pl.loop(0, NU)
    def _(b):
        rows = pl.ds(pl.multiple_of(b * ROWS, ROWS), ROWS)
        both = (dkv[rows, :].astype(F32) + OT[rows, :].astype(F32)).astype(BF16)
        KVS[rows, :] = both
        KVT[:, rows] = both.astype(F32).T.astype(BF16)

    @pl.loop(1, NU)
    def _(k):
        kv_copy(k).start()

    RKV[z, pl.ds(pl.multiple_of(c * 128, 128), 128), :] = KVS[
        pl.ds(pl.multiple_of(u * ROWS + c * 128, 128), 128), :
    ]

    @pl.loop(1, 5)
    def _(f):
        dw_block(f)

    def piece(h, st, step, part):
        rows = pl.ds(h * HALF + part * PART, PART)
        if along_x(h, st):
            j = (x + step) % 4
            return R.at[j, :, rows, :] if st == 0 else R.at[j, y, rows, :]
        j = (y + step) % 4
        return R.at[:, j, rows, :] if st == 0 else R.at[x, j, rows, :]

    def buf(h, st, slot):
        return B1.at[h, slot] if st == 0 else B2.at[h, slot]

    ROUTE = ((2, 0, 1), (2, 1, 3), (1, 1, 1), (3, 0, 3), (1, 0, 1), (3, 1, 3))

    def rcp(h, st, slot):
        step, part, to = ROUTE[slot]
        return remote(piece(h, st, step, part), buf(h, st, slot), rs.at[h, st, slot], rr.at[h, st, slot],
                      u, near(h, st, to))

    def start(h, st):
        for slot in range(4):
            rcp(h, st, slot).start()

    def pass_on(h, st):
        for slot, step, part in ((0, 1, 0), (1, 3, 1)):
            rcp(h, st, slot).wait_recv()
            p = piece(h, st, step, part)
            p[...] = p[...] + buf(h, st, slot)[...]
            rcp(h, st, slot + 4).start()

    def gather_up(h, st):
        for part, one, two in ((0, 3, 4), (1, 2, 5)):
            rcp(h, st, one).wait_recv()
            rcp(h, st, two).wait_recv()
            p = piece(h, st, 0, part)
            p[...] = p[...] + (buf(h, st, one)[...] + buf(h, st, two)[...])

    start(0, 0)

    @pl.loop(5, NU)
    def _(f):
        dw_block(f)

    for i in range(4):
        cols = pl.ds(pl.multiple_of((c * 4 + i) * 256, 256), 256)
        kvp = jnp.dot(KVT[...], N[:, :, cols].reshape(SEQ, 256), preferred_element_type=F32)
        R[:, :, 128 + (i // 2) * 16 : 144 + (i // 2) * 16, (i % 2) * 128 : (i % 2) * 128 + 128] = (
            kvp.T.reshape(4, 4, 16, 128)
        )

    start(1, 0)
    pass_on(0, 0)
    pass_on(1, 0)

    @pl.loop(1, NU)
    def _(k):
        q_copy(k).wait()
        kv_copy(k).wait()

    for i in range(2):
        a, b = RKV[2 * i], RKV[2 * i + 1]
        DP[:, QW + i * 128 : QW + (i + 1) * 128] = jnp.concatenate([a[:, 0:64], b[:, 0:64]], axis=1)
        DP[:, QW + KW + i * 128 : QW + KW + (i + 1) * 128] = jnp.concatenate([a[:, 64:], b[:, 64:]], axis=1)

    wide = tok[...].astype(F32)
    inv = lax.rsqrt(jnp.mean(wide * wide, axis=1, keepdims=True) + EPS)

    def back(f, along):
        cols = pl.ds(pl.multiple_of(f * 256, 256), 256)
        dn = lax.dot_general(DP[...], W[f // 2, pl.ds((f % 2) * 2, 2)].reshape(256, QW + 2 * KW), (((1,), (1,)), ((), ())), preferred_element_type=F32)
        unit = tok[:, cols].astype(F32) * inv
        gbuf[pl.ds(f, 1), :] = jnp.sum(dn * unit, axis=0, keepdims=True)
        scaled = dn * gain[:, cols]
        DN[f] = scaled
        return along + jnp.sum(scaled * unit, axis=1, keepdims=True)

    along = lax.fori_loop(0, NU, back, jnp.zeros((ROWS, 1), F32))
    mean = along * (1.0 / D)

    def g_copy(k):
        return remote(gbuf, GR.at[d], gs.at[k], gr.at[k], u, (d + k) % ND)

    @pl.loop(1, ND)
    def _(k):
        g_copy(k).start()

    GR[d] = gbuf[...]

    gather_up(0, 0)
    start(0, 1)
    gather_up(1, 0)
    start(1, 1)

    @pl.loop(0, NU)
    def _(f):
        cols = pl.ds(pl.multiple_of(f * 256, 256), 256)
        unit = tok[:, cols].astype(F32) * inv
        d_rows = inv * (DN[f] - unit * mean)
        dtok_o[:, cols] = (dout[:, cols].astype(F32) + d_rows).astype(BF16)

    pass_on(0, 1)
    pass_on(1, 1)

    @pl.loop(1, ND)
    def _(k):
        g_copy(k).wait()

    gsum[...] = jnp.sum(GR[...], axis=0)

    def gu_copy(k):
        return remote(gsum, GU.at[u], us.at[k], ur.at[k], (u + k) % NU, d)

    @pl.loop(1, NU)
    def _(k):
        gu_copy(k).start()

    GU[u] = gsum[...]
    gather_up(0, 1)
    gather_up(1, 1)

    def f_copy(k):
        to = (u + k) % NU
        return remote(R.at[x, y, pl.ds(pl.multiple_of(to * 16, 16), 16)], FIN.at[u], fs.at[k], fr.at[k], to, d)

    @pl.loop(1, NU)
    def _(k):
        f_copy(k).start()

    def v_block(i):
        return R.at[x, y, pl.ds(128 + (i // 2) * 16, 16), pl.ds((i % 2) * 128, 128)]

    def v_copy(i):
        return remote(v_block(i), FKV.at[z], vs.at[i], vr.at[z], c * 4 + i, d)

    def v_arrival(zs):
        return remote(v_block(0), FKV.at[zs], vs.at[0], vr.at[zs], u, d)

    for i in range(4):
        @pl.when(c * 4 + i != u)
        def _():
            v_copy(i).start()

        @pl.when(c * 4 + i == u)
        def _():
            FKV[z] = v_block(i)[...]

    FIN[u] = R[x, y, pl.ds(pl.multiple_of(u * 16, 16), 16), :]

    @pl.loop(1, NU)
    def _(k):
        gu_copy(k).wait()

    ggain_o[...] = jnp.sum(GU[...], axis=0) * FACTOR

    @pl.loop(1, NU)
    def _(k):
        f_copy(k).wait()

    for i in range(4):
        @pl.when(i * 2 + u // 4 != u)
        def _():
            v_arrival(i).wait_recv()

        @pl.when(c * 4 + i != u)
        def _():
            v_copy(i).wait_send()

    for i in range(NU):
        gqkv_o[:, i * 128 : (i + 1) * 128] = FIN[i, :, 0:128] * FACTOR
        gout_o[:, i * 128 : (i + 1) * 128] = FIN[i, :, 128:256] * FACTOR
    for i in range(2):
        a, b = FKV[2 * i] * FACTOR, FKV[2 * i + 1] * FACTOR
        gqkv_o[:, QW + i * 128 : QW + (i + 1) * 128] = jnp.concatenate([a[:, 0:64], b[:, 0:64]], axis=1)
        gqkv_o[:, QW + KW + i * 128 : QW + KW + (i + 1) * 128] = jnp.concatenate([a[:, 64:], b[:, 64:]], axis=1)

    for h in range(2):
        for st in range(2):
            for slot in range(6):
                rcp(h, st, slot).wait_send()


    for h in range(2):
        for st in range(2):
            for slot in range(6):
                w_copy(h, st, slot).wait_send()
    for a in range(2):
        own(a, 0, A, right).wait_send()
        own(a, 1, B, right).wait_send()
        own(a, 2, A, left).wait_send()
        own(a, 3, B, left).wait_send()
        fwd(a, 4, left, A, right).wait_send()
        fwd(a, 5, right, B, left).wait_send()
        own_relay(a).wait_send()
        relay(a, 0, left, A).wait_send()
        relay(a, 1, left, B).wait_send()
        relay(a, 2, right, A).wait_send()
        relay(a, 3, right, B).wait_send()
        relay(a, 4, far, A).wait_send()
        relay(a, 5, far, B).wait_send()


def block_step(tok, dout, begins, cos, sin, gain, wqkv, wout):
    dma = pltpu.SemaphoreType.DMA
    vmem = pl.BlockSpec(memory_space=pltpu.VMEM)
    V = pltpu.VMEM
    return pl.pallas_call(
        step_kernel,
        name="block_step",
        out_shape=(
            jax.ShapeDtypeStruct((ROWS, D), BF16),
            jax.ShapeDtypeStruct((16, QW + 2 * KW), F32),
            jax.ShapeDtypeStruct((16, QW), F32),
            jax.ShapeDtypeStruct((NU, 256), F32),
        ),
        in_specs=[vmem] * 8,
        out_specs=(vmem,) * 4,
        scratch_shapes=[
            V((NU, ROWS, D), BF16), V((NU, ROWS, D), BF16), V((NU, ROWS, D), BF16),
            V((4, 4, 2, 64, QW + 2 * KW), BF16), V((ND, 128, 128), BF16), V((ND, 8, 128), F32),
            V((8, 128), F32), V((1, D), F32), V((D, 256), BF16),
            V((128, SEQ), BF16), V((128, SEQ), BF16), V((SEQ, 128), BF16), V((128, SEQ), BF16),
            V((128, SEQ), BF16), V((128, SEQ), BF16), V((SEQ, 128), BF16), V((SEQ, 128), BF16),
            V((SEQ, 128), F32),
            V((ROWS, QW + 2 * KW), BF16), V((4, ROWS, 128), BF16),
            V((SEQ, 128), BF16), V((SEQ, 128), BF16), V((128, SEQ), BF16),
            V((4, 4, 2 * HALF, 256), F32), V((2, 6, 4, PART, 256), F32), V((2, 6, PART, 256), F32),
            V((NU, 16, 256), F32), V((4, 16, 128), F32), V((NU, ROWS, 256), F32),
            V((NU, 256), F32), V((ND, NU, 256), F32), V((NU, 256), F32), V((NU, NU, 256), F32),
            dma((2, 6)), dma((2, 6)), dma((2, 7)), dma((2, 7)), dma((2, 2, 6)), dma((2, 2, 6)),
            dma((ND,)), dma((ND,)), dma((ND,)), dma((ND,)), dma, dma, dma,
            dma, dma, dma((NU,)), dma((NU,)), dma((NU,)), dma((NU,)),
            dma((2, 2, 6)), dma((2, 2, 6)), dma((NU,)), dma((NU,)), dma((4,)), dma((4,)),
            dma((ND,)), dma((ND,)), dma((NU,)), dma((NU,)),
        ],
        compiler_params=pltpu.CompilerParams(
            collective_id=0, has_side_effects=True, vmem_limit_bytes=62 * 1024 * 1024
        ),
    )(tok, dout, begins, cos, sin, gain, wqkv, wout)


def body(tokens, d_out, lengths, gain, w_qkv, w_out):
    u = lax.axis_index("ulysses")
    d = lax.axis_index("dp")
    begins, places = doc_positions(lengths[0], SEQ)
    cos_t, sin_t = rotary_tables_t(places)
    d_tokens, grad_qkv, grad_out, gain_sum = block_step(
        tokens[0], d_out[0], begins[None, :], cos_t, sin_t, gain[None, :], w_qkv, w_out
    )
    grad_gain = lax.dynamic_slice(gain_sum, (u, d * 16), (1, 16)).reshape(16)
    return d_tokens[None], grad_qkv, grad_out, grad_gain


def solution(mesh):
    in_specs = (
        P("dp", "ulysses", None),
        P("dp", "ulysses", None),
        P("dp", None),
        P("dp"),
        P("dp", None),
        P("dp", None),
    )
    out_specs = (
        P("dp", "ulysses", None),
        P(("ulysses", "dp"), None),
        P(("ulysses", "dp"), None),
        P(("ulysses", "dp")),
    )
    return jax.shard_map(body, mesh=mesh, in_specs=in_specs, out_specs=out_specs, check_vma=False)
```

time: 204 us -> 134 us (0.66)
  Pallas kernels: 185 us -> 124 us
  local copies, waits for them, and re-layouts: 12 us -> 5.67 us
    pallas_call x4 -> x1, Pallas kernels: 185 us -> 124 us  [block_step(): pl.pallas_call(step_kernel, name='block_step', out_shape=(jax.ShapeDtypeS...]
    dynamic_slice x2 -> x0, local copies, waits for them, and re-layouts: 2.66 us -> none  [the longest x1 1.58 us: body(): lax.dynamic_slice_in_dim(w_full, QW + kv_head * 64, 64, axis=1)]
    unnamed x5 -> x11, local copies, waits for them, and re-layouts: 5.32 us -> 4.4 us
where the time goes in v3:
time: 134 us
  Pallas kernels  124 us (93%)
  local copies, waits for them, and re-layouts  5.67 us (4%)
  other arithmetic  3.12 us (2%)
    pallas_call x1, Pallas kernels, block_step(): pl.pallas_call(step_kernel, name='block_step', out_shape=(jax.ShapeDtypeS...  124 us
    unnamed x11, local copies, waits for them, and re-layouts  4.4 us

profile of v3, /device:TPU:1, one launch (start us, length us, event | category | flops | bytes accessed | tf_op | source)
XLA Modules:
  0.0 133.7 jit_solution(14121435834777384433)
XLA Ops:
  0.6 0.0 copy-start.3
  0.6 0.9 reduce-window_clone.1
  1.5 0.0 copy-done.3
  1.6 0.1 select_reduce_fusion
  1.7 0.0 copy-start.1
  1.7 0.6 copy-done.1
  2.3 1.0 multiply_sine_fusion
  3.3 1.1 pad_maximum_fusion
  4.4 124.2 %block_step.1 = (bf16[256,2048]{1,0:T(8,128)(2,1)}, f32[16,1536]{1,0:T(8,128)}, f32[16,1024]{1,0:T(8,128)}, f32[8,256]{1,0:T(8,128)}) custom-call(bf16[256,2048]{1,0:T(8,128)(2,1)} %bitcast.10, bf16[256,2048]{1,0:T(8,128)(2,1)} %bitcast.11, s32[1,2048]{1,0:T(1,128)} %bitcast.12, f32[64,2048]{1,0:T(8,128)} %get-tuple-element.14.cos, ...), custom_call_target="tpu_custom_call" | custom-call | tf_op jit(solution)/shard_map/block_step/pallas_call | solution.py:615
  128.6 1.3 dynamic-slice_bitcast_fusion
  129.9 0.0 copy-start
  129.9 2.3 %copy.13 = bf16[1,256,2048]{2,1,0:T(8,128)(2,1)} copy(bf16[1,256,2048]{2,1,0:T(8,128)(2,1)} %bitcast.9) | data formatting | bytes 2097152
  132.2 0.0 copy-done
  132.2 0.0 copy-start.2
  132.2 0.6 copy.14
  132.9 0.2 copy-done.2
  133.1 0.6 copy.15
  (3 shorter events, 0.0 us)
Async XLA Ops:
  0.6 0.9 copy-start.3
  1.7 0.6 copy-start.1
  129.9 2.3 %copy-start = (f32[16,1536]{1,0:T(8,128)S(1)}, f32[16,1536]{1,0:T(8,128)}, u32[]{:S(2)}) copy-start(f32[16,1536]{1,0:T(8,128)} %get-tuple-element.21) | copy-start | bytes 294916
  132.2 0.9 copy-start.2

commit v4 on v3

--- a/solution.py
+++ b/solution.py
@@ -25,7 +25,8 @@
 
 
 def doc_positions(doc_lengths, length):
-    bounds = jnp.cumsum(doc_lengths) - doc_lengths
+    order = jnp.arange(doc_lengths.shape[0])
+    bounds = jnp.sum(jnp.where(order[None, :] < order[:, None], doc_lengths[None, :], 0), axis=1)
     places = jnp.arange(length, dtype=jnp.int32)
     begins = jnp.max(jnp.where(bounds[None, :] <= places[:, None], bounds[None, :], 0), axis=1)
     return begins, places - begins
@@ -34,8 +35,7 @@
 def rotary_tables_t(places):
     inverse = ROPE_BASE ** (-jnp.arange(0, HEAD_DIM, 2).astype(F32) / HEAD_DIM)
     angles = inverse[:, None] * places.astype(F32)[None, :]
-    cos, sin = jnp.cos(angles), jnp.sin(angles)
-    return jnp.concatenate([cos, cos], axis=0), jnp.concatenate([sin, sin], axis=0)
+    return jnp.cos(angles), jnp.sin(angles)
 
 
 def remote(src, dst, send_sem, recv_sem, u, d):
@@ -53,8 +53,8 @@
 
 
 def rot_t(u, cos, sin):
-    half = HEAD_DIM // 2
-    return u * cos + jnp.concatenate([-u[half:], u[:half]], axis=0) * sin
+    a, b = u[: HEAD_DIM // 2], u[HEAD_DIM // 2 :]
+    return jnp.concatenate([a * cos - b * sin, b * cos + a * sin], axis=0)
 
 
 def step_kernel(tok, dout, begins, cos, sin, gain_in, wqkv, wout,
@@ -212,13 +212,13 @@
         kv_t[:, cols] = both.astype(BF16)
         kv[cols, :] = both.T.astype(BF16)
 
-    def attend(ch):
-        da_t[:, chunk_cols(ch)] = jnp.dot(
-            G[ch], WO[...].reshape(D, 128), preferred_element_type=F32
-        ).T.astype(BF16)
-
-        @pl.loop(ch * 2, ch * 2 + 2)
-        def _(i):
+    def attend(*blocks):
+        for i in blocks:
+            da_t[:, pl.ds(pl.multiple_of(i * QB, QB), QB)] = jnp.dot(
+                G[i // 2, pl.ds(pl.multiple_of((i % 2) * QB, QB), QB), :], WO[...].reshape(D, 128),
+                preferred_element_type=F32,
+            ).T.astype(BF16)
+        for i in blocks:
             attend_block(i)
 
     def attend_block(i):
@@ -329,15 +329,38 @@
 
     @pl.loop(0, 2)
     def _(n):
-        attend(z * 2 + n)
-
+        attend((z * 2 + n) * 2, (z * 2 + n) * 2 + 1)
+
+    def attend_near(first):
+        @pl.loop(0, 2)
+        def _(n):
+            base = ((z + 3 + 2 * n) % 4) * 4
+            half = n if first else 1 - n
+            attend(base + half, base + 2 + half)
+
+    relay(1, 0, left, A).wait_recv()
+    relay(1, 3, left, B).wait_recv()
+    attend_near(True)
     late(1)
-    for slot, rows in ((0, A), (1, B), (2, A), (3, B)):
-        relay(1, slot, left, rows).wait_recv()
-
-    @pl.loop(0, 4)
-    def _(n):
-        attend(((z + 1 + 2 * (n // 2)) % 4) * 2 + n % 2)
+    relay(1, 1, left, B).wait_recv()
+    relay(1, 2, left, A).wait_recv()
+    attend_near(False)
+
+    def dw(f, steps, add):
+        cols = pl.ds(pl.multiple_of(f * 256, 256), 256)
+        q = o = 0.0
+        for step in steps:
+            zz = (z + step) % 4
+            toks = pl.ds(pl.multiple_of(zz * 512, 512), 512)
+            q += jnp.dot(dq_t[:, toks], N[pl.ds(zz * 2, 2), :, cols].reshape(512, 256), preferred_element_type=F32)
+            o += jnp.dot(attn_t[:, toks], G[pl.ds(zz * 2, 2), :, cols].reshape(512, 256), preferred_element_type=F32)
+        rows = pl.ds(pl.multiple_of(f * 16, 16), 16)
+        both = jnp.concatenate([q.T, o.T], axis=1).reshape(4, 4, 16, 256)
+        R[:, :, rows, :] = R[:, :, rows, :] + both if add else both
+
+    @pl.loop(0, NU)
+    def _(f):
+        dw(f, (0, 1, 3), False)
 
     last(1)
 
@@ -348,7 +371,8 @@
             relay(1, 4, far, A).wait_recv()
             relay(1, 5, far, B).wait_recv()
 
-        attend(((z + 2) % 4) * 2 + (c + n) % 2)
+        ch = ((z + 2) % 4) * 2 + (c + n) % 2
+        attend(ch * 2, ch * 2 + 1)
 
     @pl.loop(0, NU)
     def _(b):
@@ -376,37 +400,6 @@
         q_copy(k).start()
 
     DP[:, pl.ds(pl.multiple_of(u * 128, 128), 128)] = dq[pl.ds(pl.multiple_of(u * ROWS, ROWS), ROWS), :]
-
-    def dw_block(f):
-        cols = pl.ds(pl.multiple_of(f * 256, 256), 256)
-        rows = pl.ds(pl.multiple_of(f * 16, 16), 16)
-        q = jnp.dot(dq_t[...], N[:, :, cols].reshape(SEQ, 256), preferred_element_type=F32)
-        R[:, :, rows, 0:128] = q.T.reshape(4, 4, 16, 128)
-        o = jnp.dot(attn_t[...], G[:, :, cols].reshape(SEQ, 256), preferred_element_type=F32)
-        R[:, :, rows, 128:256] = o.T.reshape(4, 4, 16, 128)
-
-    dw_block(0)
-
-    m_copy.wait()
-
-    @pl.loop(0, NU)
-    def _(b):
-        rows = pl.ds(pl.multiple_of(b * ROWS, ROWS), ROWS)
-        both = (dkv[rows, :].astype(F32) + OT[rows, :].astype(F32)).astype(BF16)
-        KVS[rows, :] = both
-        KVT[:, rows] = both.astype(F32).T.astype(BF16)
-
-    @pl.loop(1, NU)
-    def _(k):
-        kv_copy(k).start()
-
-    RKV[z, pl.ds(pl.multiple_of(c * 128, 128), 128), :] = KVS[
-        pl.ds(pl.multiple_of(u * ROWS + c * 128, 128), 128), :
-    ]
-
-    @pl.loop(1, 5)
-    def _(f):
-        dw_block(f)
 
     def piece(h, st, step, part):
         rows = pl.ds(h * HALF + part * PART, PART)
@@ -444,11 +437,32 @@
             p = piece(h, st, 0, part)
             p[...] = p[...] + (buf(h, st, one)[...] + buf(h, st, two)[...])
 
+    @pl.loop(0, 5)
+    def _(f):
+        dw(f, (2,), True)
+
     start(0, 0)
 
     @pl.loop(5, NU)
     def _(f):
-        dw_block(f)
+        dw(f, (2,), True)
+
+    m_copy.wait()
+
+    @pl.loop(0, NU)
+    def _(b):
+        rows = pl.ds(pl.multiple_of(b * ROWS, ROWS), ROWS)
+        both = (dkv[rows, :].astype(F32) + OT[rows, :].astype(F32)).astype(BF16)
+        KVS[rows, :] = both
+        KVT[:, rows] = both.astype(F32).T.astype(BF16)
+
+    @pl.loop(1, NU)
+    def _(k):
+        kv_copy(k).start()
+
+    RKV[z, pl.ds(pl.multiple_of(c * 128, 128), 128), :] = KVS[
+        pl.ds(pl.multiple_of(u * ROWS + c * 128, 128), 128), :
+    ]
 
     for i in range(4):
         cols = pl.ds(pl.multiple_of((c * 4 + i) * 256, 256), 256)

time: 134 us -> 128 us (0.955)
  Pallas kernels: 124 us -> 119 us
    pallas_call x1, Pallas kernels: 124 us -> 119 us  [block_step(): pl.pallas_call(step_kernel, name='block_step', out_shape=(jax.ShapeDtypeS...]
where the time goes in v4:
time: 128 us
  Pallas kernels  119 us (93%)
  local copies, waits for them, and re-layouts  6.33 us (5%)
  other arithmetic  2.04 us (2%)
    pallas_call x1, Pallas kernels, block_step(): pl.pallas_call(step_kernel, name='block_step', out_shape=(jax.ShapeDtypeS...  119 us
    unnamed x11, local copies, waits for them, and re-layouts  5.06 us

profile of v4, /device:TPU:1, one launch (start us, length us, event | category | flops | bytes accessed | tf_op | source)
XLA Modules:
  0.0 128.0 jit_solution(15748091349868886316)
XLA Ops:
  0.6 0.0 copy-start.3
  0.6 0.6 copy-done.3
  1.3 0.1 select_reduce_fusion.1
  1.4 0.1 select_reduce_fusion
  1.5 0.0 copy-start.1
  1.6 0.6 copy-done.1
  2.1 1.8 %multiply_sine_fusion = (f32[32,2048]{1,0:T(8,128)}, f32[32,2048]{1,0:T(8,128)}) fusion(f32[2048]{0:T(1024)S(1)} %subtract_convert_fusion, f32[32]{0:T(128)S(1)} %multiply_power_fusion), kind=kLoop, calls=%fused_computation | loop fusion | flops 65536 | bytes 532608 | tf_op jit(solution)/shard_map/sin | solution.py:38
  3.9 119.0 %block_step.1 = (bf16[256,2048]{1,0:T(8,128)(2,1)}, f32[16,1536]{1,0:T(8,128)}, f32[16,1024]{1,0:T(8,128)}, f32[8,256]{1,0:T(8,128)}) custom-call(bf16[256,2048]{1,0:T(8,128)(2,1)} %bitcast.8, bf16[256,2048]{1,0:T(8,128)(2,1)} %bitcast.9, s32[1,2048]{1,0:T(1,128)} %bitcast.11, f32[32,2048]{1,0:T(8,128)} %get-tuple-element.13.cos, ...), custom_call_target="tpu_custom_call" | custom-call | tf_op jit(solution)/shard_map/block_step/pallas_call | solution.py:629
  122.9 1.3 dynamic-slice_bitcast_fusion
  124.2 0.0 copy-start
  124.2 2.3 %copy.13 = bf16[1,256,2048]{2,1,0:T(8,128)(2,1)} copy(bf16[1,256,2048]{2,1,0:T(8,128)(2,1)} %bitcast.10) | data formatting | bytes 2097152
  126.5 0.0 copy-done
  126.6 0.0 copy-start.2
  126.6 0.6 copy.14
  127.2 0.2 copy-done.2
  127.4 0.6 copy.15
  (2 shorter events, 0.0 us)
Async XLA Ops:
  0.6 0.7 copy-start.3
  1.5 0.6 copy-start.1
  124.2 2.3 %copy-start = (f32[16,1536]{1,0:T(8,128)S(1)}, f32[16,1536]{1,0:T(8,128)}, u32[]{:S(2)}) copy-start(f32[16,1536]{1,0:T(8,128)} %get-tuple-element.19) | copy-start | bytes 294916
  126.6 0.9 copy-start.2

commit v5 on v4

--- a/solution.py
+++ b/solution.py
@@ -402,7 +402,7 @@
     DP[:, pl.ds(pl.multiple_of(u * 128, 128), 128)] = dq[pl.ds(pl.multiple_of(u * ROWS, ROWS), ROWS), :]
 
     def piece(h, st, step, part):
-        rows = pl.ds(h * HALF + part * PART, PART)
+        rows = pl.ds(h * HALF, HALF) if st == 1 else pl.ds(h * HALF + part * PART, PART)
         if along_x(h, st):
             j = (x + step) % 4
             return R.at[j, :, rows, :] if st == 0 else R.at[j, y, rows, :]
@@ -415,12 +415,15 @@
     ROUTE = ((2, 0, 1), (2, 1, 3), (1, 1, 1), (3, 0, 3), (1, 0, 1), (3, 1, 3))
 
     def rcp(h, st, slot):
+        if st == 1:
+            step = slot + 1
+            return remote(piece(h, 1, step, 0), buf(h, 1, slot), rs.at[h, 1, slot], rr.at[h, 1, slot], u, near(h, 1, step))
         step, part, to = ROUTE[slot]
         return remote(piece(h, st, step, part), buf(h, st, slot), rs.at[h, st, slot], rr.at[h, st, slot],
                       u, near(h, st, to))
 
     def start(h, st):
-        for slot in range(4):
+        for slot in range(4 if st == 0 else 3):
             rcp(h, st, slot).start()
 
     def pass_on(h, st):
@@ -431,6 +434,12 @@
             rcp(h, st, slot + 4).start()
 
     def gather_up(h, st):
+        if st == 1:
+            for slot in range(3):
+                rcp(h, 1, slot).wait_recv()
+            p = piece(h, 1, 0, 0)
+            p[...] = p[...] + (buf(h, 1, 0)[...] + buf(h, 1, 1)[...] + buf(h, 1, 2)[...])
+            return
         for part, one, two in ((0, 3, 4), (1, 2, 5)):
             rcp(h, st, one).wait_recv()
             rcp(h, st, two).wait_recv()
@@ -521,8 +530,6 @@
         d_rows = inv * (DN[f] - unit * mean)
         dtok_o[:, cols] = (dout[:, cols].astype(F32) + d_rows).astype(BF16)
 
-    pass_on(0, 1)
-    pass_on(1, 1)
 
     @pl.loop(1, ND)
     def _(k):
@@ -598,7 +605,7 @@
 
     for h in range(2):
         for st in range(2):
-            for slot in range(6):
+            for slot in range(6 if st == 0 else 3):
                 rcp(h, st, slot).wait_send()
 
 
@@ -646,7 +653,7 @@
             V((SEQ, 128), F32),
             V((ROWS, QW + 2 * KW), BF16), V((4, ROWS, 128), BF16),
             V((SEQ, 128), BF16), V((SEQ, 128), BF16), V((128, SEQ), BF16),
-            V((4, 4, 2 * HALF, 256), F32), V((2, 6, 4, PART, 256), F32), V((2, 6, PART, 256), F32),
+            V((4, 4, 2 * HALF, 256), F32), V((2, 6, 4, PART, 256), F32), V((2, 3, HALF, 256), F32),
             V((NU, 16, 256), F32), V((4, 16, 128), F32), V((NU, ROWS, 256), F32),
             V((NU, 256), F32), V((ND, NU, 256), F32), V((NU, 256), F32), V((NU, NU, 256), F32),
             dma((2, 6)), dma((2, 6)), dma((2, 7)), dma((2, 7)), dma((2, 2, 6)), dma((2, 2, 6)),

time: 128 us -> 128 us (level)
  no operation moved by 1% of the time
where the time goes in v5:
time: 128 us
  Pallas kernels  119 us (93%)
  local copies, waits for them, and re-layouts  6.33 us (5%)
  other arithmetic  2.04 us (2%)
    pallas_call x1, Pallas kernels, block_step(): pl.pallas_call(step_kernel, name='block_step', out_shape=(jax.ShapeDtypeS...  119 us
    unnamed x11, local copies, waits for them, and re-layouts  5.06 us

profile of v5, /device:TPU:1, one launch (start us, length us, event | category | flops | bytes accessed | tf_op | source)
XLA Modules:
  0.0 127.6 jit_solution(6700016162683145497)
XLA Ops:
  0.6 0.0 copy-start.3
  0.6 0.6 copy-done.3
  1.3 0.1 select_reduce_fusion.1
  1.4 0.1 select_reduce_fusion
  1.5 0.0 copy-start.1
  1.6 0.6 copy-done.1
  2.1 1.8 %multiply_sine_fusion = (f32[32,2048]{1,0:T(8,128)}, f32[32,2048]{1,0:T(8,128)}) fusion(f32[2048]{0:T(1024)S(1)} %subtract_convert_fusion, f32[32]{0:T(128)S(1)} %multiply_power_fusion), kind=kLoop, calls=%fused_computation | loop fusion | flops 65536 | bytes 532608 | tf_op jit(solution)/shard_map/sin | solution.py:38
  3.9 118.6 %block_step.1 = (bf16[256,2048]{1,0:T(8,128)(2,1)}, f32[16,1536]{1,0:T(8,128)}, f32[16,1024]{1,0:T(8,128)}, f32[8,256]{1,0:T(8,128)}) custom-call(bf16[256,2048]{1,0:T(8,128)(2,1)} %bitcast.8, bf16[256,2048]{1,0:T(8,128)(2,1)} %bitcast.9, s32[1,2048]{1,0:T(1,128)} %bitcast.11, f32[32,2048]{1,0:T(8,128)} %get-tuple-element.13.cos, ...), custom_call_target="tpu_custom_call" | custom-call | tf_op jit(solution)/shard_map/block_step/pallas_call | solution.py:636
  122.5 1.3 dynamic-slice_bitcast_fusion
  123.8 0.0 copy-start
  123.8 2.3 %copy.13 = bf16[1,256,2048]{2,1,0:T(8,128)(2,1)} copy(bf16[1,256,2048]{2,1,0:T(8,128)(2,1)} %bitcast.10) | data formatting | bytes 2097152
  126.2 0.0 copy-done
  126.2 0.0 copy-start.2
  126.2 0.6 copy.14
  126.8 0.2 copy-done.2
  127.0 0.6 copy.15
  (2 shorter events, 0.0 us)
Async XLA Ops:
  0.6 0.7 copy-start.3
  1.5 0.6 copy-start.1
  123.8 2.3 %copy-start = (f32[16,1536]{1,0:T(8,128)S(1)}, f32[16,1536]{1,0:T(8,128)}, u32[]{:S(2)}) copy-start(f32[16,1536]{1,0:T(8,128)} %get-tuple-element.19) | copy-start | bytes 294916
  126.2 0.9 copy-start.2
